TPU v7x, 32 devices: a whole 2x2x4 slice. The times are simulated.
32 devices in a mesh: slab: 2 (over x), blk: 16 (over z, y, core).
Axes of the slice: x: 2, y: 2, z: 4, core: 2. Of those that a mesh axis runs over, the one named last changes fastest.
Arguments:
- transmit: bfloat16 [2, 1024, 2048], P('slab', 'blk'), may hold values from -0.125 to 0.125
- reflect: bfloat16 [2, 2, 1024, 2048], P('slab', None, 'blk'), may hold values from -0.07910156 to 0.07910156
- source_amp: bfloat16 [512, 2048], P('blk'), may hold values from -6 to 6
- source_cell: int32 [512], P('blk'), may hold values from 0 to 1023
- source_slab: int32 [512], P('blk'), may hold values from 0 to 1
Outputs:
- sweep_out: float32 [2, 512, 2048], P('slab', 'blk')
All inputs are finite; a program needn't handle non-finite values.
Results may differ from a plain program's by a relative error of at most 0.018.
Values may be sent and summed in bfloat16 or wider, within the bound.
A program may use at most 64 MiB of HBM per device.

v0:
```python
import functools

import jax
import jax.numpy as jnp
from jax import lax
from jax.experimental import pallas as pl
from jax.experimental.pallas import tpu as pltpu
from jax.sharding import PartitionSpec as P


def shifted(block, axis, distance):
    devices = range(lax.axis_size(axis))
    route = [(i - distance, i) for i in devices if i - distance in devices]
    return lax.ppermute(block, axis, route)


def transposed(matrix):
    half_width = matrix.shape[0]
    return jnp.concatenate([matrix[:, :half_width].T, matrix[:, half_width:].T], 1)


def complex_rows(left_rows, right_matrix):
    inner_width = right_matrix.shape[0]
    outer_width = right_matrix.shape[1] // 2
    row_count = left_rows.shape[0]
    stacked = jnp.concatenate([left_rows[:, :inner_width], left_rows[:, inner_width:]], 0)
    product = jnp.dot(stacked, right_matrix, preferred_element_type=jnp.float32)
    real_out = product[:row_count, :outer_width] - product[row_count:, outer_width:]
    imag_out = product[:row_count, outer_width:] + product[row_count:, :outer_width]
    return jnp.concatenate([real_out, imag_out], 1)


def body(transmit, reflect, source_amp, source_cell, source_slab):
    trans_local = transmit[0]
    refl_local = reflect[0]
    half_width = source_amp.shape[1] // 2
    refl_second = lax.all_gather(refl_local[1], "blk", axis=0, tiled=True)
    coupling = complex_rows(refl_local[0], refl_second).astype(jnp.bfloat16)
    start_rows = trans_local.astype(jnp.float32)
    piece_rows = lax.all_gather(trans_local, "blk", axis=0, tiled=True)
    piece_count = piece_rows.shape[0]
    real_cols = lax.slice_in_dim(coupling, 0, piece_count, axis=1)
    imag_cols = lax.dynamic_slice_in_dim(coupling, half_width, piece_count, 1)
    left_rows = jnp.concatenate([real_cols, imag_cols], 1)
    joined = (start_rows + complex_rows(left_rows, piece_rows)).astype(jnp.bfloat16)
    slab_matrix = lax.all_gather(joined, "blk", axis=0, tiled=True)
    back_matrix = transposed(slab_matrix)
    cell_index = lax.iota(jnp.int32, half_width)
    offset = (cell_index[None, :] - source_cell[:, None]) % half_width
    inside = offset < half_width // 4
    here = source_slab == lax.axis_index("slab")
    keep = inside & here[:, None]
    keep = jnp.concatenate([keep, keep], 1)
    forcing = jnp.where(keep, source_amp, jnp.zeros_like(source_amp))
    chain_length = lax.axis_size("slab")
    carried = forcing
    for sweep_step in range(chain_length - 1):
        arrived = shifted(carried, "slab", 1)
        carried = (forcing.astype(jnp.float32) + complex_rows(arrived, slab_matrix)).astype(
            jnp.bfloat16
        )
    current = carried.astype(jnp.float32)
    for sweep_step in range(chain_length - 1):
        message = complex_rows(current.astype(jnp.bfloat16), back_matrix).astype(jnp.bfloat16)
        arrived = shifted(message, "slab", -1)
        current = carried.astype(jnp.float32) + arrived.astype(jnp.float32)
    return current[None]


MESH = pl.DeviceIdType.MESH
Y = 2
CORE = 2
PLANES = 2


def pair_kernel(
    outer, t_hbm, r_hbm, amp_hbm, cell_hbm, slab_hbm, out_ref,
    amp_ref, cell_ref, slab_ref, g_ref, left_ref, coup_ref, x_ref, base_ref,
    f_ref, whole_ref, d_ref, far_ref,
    arg_sem, in_send, in_recv, left_send, left_recv, z_send, z_recv,
    c_send, c_recv, x_send, x_recv, f_send, f_recv, d_send, d_recv,
):
    plane = lax.axis_index("slab")
    me = lax.axis_index("blk")
    z, y, core = me // (Y * CORE), (me // CORE) % Y, me % CORE
    last = PLANES - 1
    depth = t_hbm.shape[1]
    width = t_hbm.shape[2] // 2
    part_width = width // (PLANES * Y)
    sources = amp_hbm.shape[0]
    y_peer, c_peer, x_peer = 1 - y, 1 - core, 1 - plane
    q = plane * Y + y
    f32, bf16 = jnp.float32, jnp.bfloat16

    def dev(p, zz, yy, cc):
        return (p, (zz * Y + yy) * CORE + cc)

    def cols(quarter, base=0):
        return pl.ds(pl.multiple_of(base + quarter * part_width, part_width), part_width)

    def remote(s, d, ss, rs, to):
        return pltpu.make_async_remote_copy(
            src_ref=s, dst_ref=d, send_sem=ss, recv_sem=rs, device_id=to, device_id_type=MESH)

    def piece(m, part, p, yy):
        s = r_hbm.at[0, 1] if m == 0 else t_hbm.at[0]
        return s.at[:, cols(p * Y + yy, part * width)]

    def slot(m, part, yy):
        return g_ref.at[m, part].at[z * Y + yy, core]

    def piece_local(m, part):
        return pltpu.make_async_copy(piece(m, part, last, y), slot(m, part, y), in_recv.at[(m * 2 + part) * Y + y])

    targets = ((0, y), (0, y_peer), (last, y_peer))

    def piece_send(m, part, k):
        p, yy = targets[k]
        return remote(piece(m, part, p, yy), slot(m, part, y), in_send.at[m, part, k],
                      in_recv.at[(m * 2 + part) * Y + y], dev(p, z, yy, core))

    def piece_recv(m, part, yy):
        return remote(slot(m, part, yy), slot(m, part, yy), in_send.at[m, part, 0],
                      in_recv.at[(m * 2 + part) * Y + yy], dev(plane, z, y_peer, core))

    def left_src(part):
        return r_hbm.at[0, 0, :, part * width:(part + 1) * width]

    def left_local(part):
        return pltpu.make_async_copy(left_src(part), left_ref.at[part].at[y], left_recv.at[part * Y + y])

    def left_push(part, k):
        to = dev(0, z, y, core) if k == 0 else dev(last, z, y_peer, core)
        return remote(left_src(part), left_ref.at[part].at[y], left_send.at[part, k],
                      left_recv.at[part * Y + y], to)

    def left_relay(part, yy):
        ref = left_ref.at[part].at[yy]
        return remote(ref, ref, left_send.at[part, 0], left_recv.at[part * Y + yy],
                      dev(plane, z, y_peer, core))

    args = [pltpu.make_async_copy(a, b, arg_sem.at[i]) for i, (a, b) in enumerate(
        ((amp_hbm, amp_ref), (cell_hbm, cell_ref), (slab_hbm, slab_ref)))]
    for copy in args:
        copy.start()

    @pl.when(plane == last)
    def _():
        for m in range(2):
            for part in range(2):
                piece_local(m, part).start()
        for part in range(2):
            left_local(part).start()

    barrier = pltpu.get_barrier_semaphore()
    peers = [dev(plane, (z + step) % outer, y, core) for step in range(1, outer)]
    peers += [dev(plane, z, y, c_peer), dev(plane, z, y_peer, core),
              dev(x_peer, z, y, core), dev(x_peer, z, y_peer, core)]
    for peer in peers:
        pl.semaphore_signal(barrier, inc=1, device_id=peer, device_id_type=MESH)
    pl.semaphore_wait(barrier, len(peers))

    @pl.when(plane == last)
    def _():
        for part in range(2):
            for k in range(3):
                piece_send(0, part, k).start()
        for part in range(2):
            for k in range(2):
                left_push(part, k).start()
        for part in range(2):
            for k in range(3):
                piece_send(1, part, k).start()

    def pieces_ready(m):
        for part in range(2):
            @pl.when(plane == last)
            def _():
                piece_local(m, part).wait()

            @pl.when(plane != last)
            def _():
                piece_recv(m, part, y).wait_recv()

            piece_recv(m, part, y_peer).wait_recv()

    pending = []
    always = plane >= 0
    steps = [s for d in range(1, outer) for s in (d, -d)]
    near = [s for s in steps if abs(s) <= 2]

    def chunk(m, zz, cc):
        return g_ref.at[m].at[:, pl.ds(zz * Y, Y), cc]

    def push(m, k, shift, to, ok):
        zz = z + shift
        ref = chunk(m, zz, core)
        copy = remote(ref, ref, z_send.at[m, k], z_recv.at[(m * outer + zz) * CORE + core], to)
        copy.start()
        pending.append((ok, m, k, shift))

    def landed(m, zz, cc):
        ref = chunk(m, zz, cc)
        remote(ref, ref, z_send.at[m, 0], z_recv.at[(m * outer + zz) * CORE + cc],
               dev(plane, z, y, c_peer)).wait_recv()

    def valid(zz):
        return (zz >= 0) & (zz < outer)

    def spread_own(m):
        for k, s in enumerate(sorted(near, key=lambda v: -abs(v))):
            ok = valid(z + s)

            @pl.when(ok)
            def _():
                push(m, k, 0, dev(plane, z + s, y, core), ok)
        push(m, 4, 0, dev(plane, z, y, c_peer), always)

    def spread(m, chosen):
        for s in chosen:
            i = steps.index(s)
            ok = valid(z + s)

            @pl.when(ok)
            def _():
                landed(m, z + s, core)
            if abs(s) >= 2:
                onward = 1 if s < 0 else -1
                both = ok & valid(z + onward)

                @pl.when(both)
                def _():
                    push(m, 5 + len(steps) + i, s, dev(plane, z + onward, y, core), both)

            @pl.when(ok)
            def _():
                push(m, 5 + i, s, dev(plane, z, y, c_peer), ok)

    def finish(m):
        for zz in range(outer):
            landed(m, zz, c_peer)

    def side(m, part):
        return g_ref[m, part].reshape(width, part_width)

    def complex_rows_here(lhs, m):
        n = lhs.shape[0] // 2
        pr = jnp.dot(lhs, side(m, 0), preferred_element_type=f32)
        pi = jnp.dot(lhs, side(m, 1), preferred_element_type=f32)
        return pr[:n] - pi[n:], pi[:n] + pr[n:]

    seconds = [s for s in steps if abs(s) == 2]
    firsts = [s for s in steps if abs(s) == 1]
    rest = [s for s in steps if abs(s) > 2]

    for copy in args:
        copy.wait()
    eye = (lax.broadcasted_iota(jnp.int32, (sources, sources), 0)
           == lax.broadcasted_iota(jnp.int32, (sources, sources), 1))
    cell = jnp.sum(jnp.where(eye, cell_ref[...], 0), axis=1, keepdims=True)
    slab = jnp.sum(jnp.where(eye, slab_ref[...], 0), axis=1, keepdims=True)
    offset = lax.broadcasted_iota(jnp.int32, (sources, width), 1) - cell
    offset = jnp.where(offset < 0, offset + width, offset)
    inside = offset < width // 4
    for part in range(2):
        amp = amp_ref[:, part * width:(part + 1) * width].astype(f32)
        x_ref[part, y] = jnp.where(inside & (slab == 0), amp, 0.0).astype(bf16)
        base_ref[part, y] = jnp.where(inside & (slab == 1), amp, 0.0).astype(bf16)

    pieces_ready(0)
    spread_own(0)

    def x_swap(yy):
        ref = x_ref.at[:, yy]
        return remote(ref, ref, x_send.at[0], x_recv.at[0], dev(plane, z, y_peer, core))

    def base_swap(yy, quarter):
        ref = base_ref.at[:, yy, :, cols(quarter)]
        return remote(ref, ref, x_send.at[1], x_recv.at[1], dev(plane, z, y_peer, core))

    x_swap(y).start()
    base_swap(y, plane * Y + y_peer).start()

    for part in range(2):
        @pl.when(plane == last)
        def _():
            left_local(part).wait()

        @pl.when(plane != last)
        def _():
            left_relay(part, y).wait_recv()
            left_relay(part, y).start()

    spread(0, seconds)
    pieces_ready(1)
    spread_own(1)
    spread(0, firsts + rest)
    finish(0)
    for part in range(2):
        left_relay(part, y_peer).wait_recv()

    re, im = complex_rows_here(left_ref[...].reshape(2 * Y * depth, width), 0)
    coup_ref[0:Y * depth, cols(q)] = re.astype(bf16)
    coup_ref[Y * depth:, cols(q)] = im.astype(bf16)
    others = ((x_peer, y), (plane, y_peer), (x_peer, y_peer))

    def coup_copy(k, quarter):
        p, yy = others[k]
        ref = coup_ref.at[:, cols(quarter)]
        return remote(ref, ref, c_send.at[k], c_recv.at[quarter], dev(p, z, yy, core))

    for k in range(3):
        coup_copy(k, q).start()
    spread(1, seconds + firsts + rest)
    finish(1)
    for k, (p, yy) in enumerate(others):
        coup_copy(k, p * Y + yy).wait_recv()

    re, im = complex_rows_here(coup_ref[...], 1)
    for part, value in ((0, re), (1, im)):
        start = g_ref[1, part, pl.ds(z * Y, Y), core].reshape(Y * depth, part_width)
        joined = (value + start.astype(f32)).astype(bf16)
        g_ref[2, part, pl.ds(z * Y, Y), core] = joined.reshape(Y, depth, part_width)
    spread_own(2)
    spread(2, seconds + firsts + rest)
    x_swap(y_peer).wait_recv()
    base_swap(y_peer, q).wait_recv()
    finish(2)

    re, im = complex_rows_here(x_ref[...].reshape(2 * Y * sources, width), 2)
    for part, value in ((0, re), (1, im)):
        start = base_ref[part, :, :, cols(q)].astype(f32)
        f_ref[part] = (value.reshape(Y, sources, part_width) + start).astype(bf16)

    lhs = f_ref[...].reshape(2 * Y * sources, part_width)
    n = Y * sources
    tile = Y * CORE * depth

    def d_copy(k, yy, quarter, j):
        spots = slice(j * tile, (j + 1) * tile)
        return remote(d_ref.at[:, yy, :, spots], far_ref.at[quarter].at[:, :, spots],
                      d_send.at[k, j], d_recv.at[quarter * outer + j], dev(0, z, yy, core))

    def f_copy(k, yy, quarter):
        return remote(f_ref.at[:, yy], whole_ref.at[:, :, cols(quarter)], f_send.at[k],
                      f_recv.at[quarter], dev(last, z, yy, core))

    for j in range(outer):
        spots = slice(j * tile, (j + 1) * tile)
        dims = (((1,), (1,)), ((), ()))
        right = [g_ref[2, part, j * Y:(j + 1) * Y].reshape(tile, part_width) for part in range(2)]
        pr = lax.dot_general(lhs, right[0], dims, preferred_element_type=f32)
        pi = lax.dot_general(lhs, right[1], dims, preferred_element_type=f32)
        d_ref[0, :, :, spots] = (pr[:n] - pi[n:]).astype(bf16).reshape(Y, sources, tile)
        d_ref[1, :, :, spots] = (pi[:n] + pr[n:]).astype(bf16).reshape(Y, sources, tile)
        d_copy(0, y_peer, q, j).start()

        @pl.when(plane == last)
        def _():
            d_copy(1, y, q, j).start()

    f_copy(0, y_peer, q).start()

    @pl.when(plane != last)
    def _():
        f_copy(1, y, q).start()

    @pl.when(plane == last)
    def _():
        whole_ref[:, :, cols(q)] = f_ref[:, y]
        for p, yy in others:
            f_copy(0, y, p * Y + yy).wait_recv()
        for part in range(2):
            out_ref[:, part * width:(part + 1) * width] = whole_ref[part].astype(f32)

    @pl.when(plane != last)
    def _():
        for j in range(outer):
            spots = slice(j * tile, (j + 1) * tile)
            for p, yy in others:
                d_copy(0, y, p * Y + yy, j).wait_recv()
            for part in range(2):
                total = d_ref.at[part][y, :, spots].astype(f32)
                for p, yy in others:
                    total = total + far_ref.at[p * Y + yy][part, :, spots].astype(f32)
                out_ref[:, part * width + j * tile:part * width + (j + 1) * tile] = (
                    x_ref.at[part][y, :, spots].astype(f32) + total.astype(bf16).astype(f32))

    @pl.when(plane == last)
    def _():
        for j in range(outer):
            d_copy(1, y, q, j).wait_send()
        for m in range(2):
            for part in range(2):
                for k in range(3):
                    piece_send(m, part, k).wait_send()
        for part in range(2):
            for k in range(2):
                left_push(part, k).wait_send()

    @pl.when(plane != last)
    def _():
        f_copy(1, y, q).wait_send()
        for part in range(2):
            left_relay(part, y).wait_send()

    for j in range(outer):
        d_copy(0, y_peer, q, j).wait_send()
    f_copy(0, y_peer, q).wait_send()
    x_swap(y).wait_send()
    base_swap(y, plane * Y + y_peer).wait_send()
    for k in range(3):
        coup_copy(k, q).wait_send()
    for ok, m, k, shift in pending:
        @pl.when(ok)
        def _():
            ref = chunk(m, z + shift, core)
            remote(ref, ref, z_send.at[m, k], z_recv.at[(m * outer + z + shift) * CORE + core],
                   dev(plane, z, y, c_peer)).wait_send()


def pair_body(transmit, reflect, source_amp, source_cell, source_slab):
    outer = lax.axis_size("blk") // (Y * CORE)
    sources, double = source_amp.shape
    depth = transmit.shape[1]
    width = double // 2
    quarter = width // (PLANES * Y)
    bf16 = jnp.bfloat16
    hbm = pl.BlockSpec(memory_space=pltpu.HBM)
    sem = pltpu.SemaphoreType.DMA
    out = pl.pallas_call(
        functools.partial(pair_kernel, outer),
        out_shape=jax.ShapeDtypeStruct((sources, double), jnp.float32),
        in_specs=[hbm] * 5,
        out_specs=pl.BlockSpec(memory_space=pltpu.VMEM),
        scratch_shapes=[
            pltpu.VMEM((sources, double), bf16),
            pltpu.VMEM((1, sources), jnp.int32),
            pltpu.VMEM((1, sources), jnp.int32),
            pltpu.VMEM((3, 2, outer * Y, CORE, depth, quarter), bf16),
            pltpu.VMEM((2, Y, depth, width), bf16),
            pltpu.VMEM((2 * Y * depth, width), bf16),
            pltpu.VMEM((2, Y, sources, width), bf16),
            pltpu.VMEM((2, Y, sources, width), bf16),
            pltpu.VMEM((2, Y, sources, quarter), bf16),
            pltpu.VMEM((2, sources, width), bf16),
            pltpu.VMEM((2, Y, sources, width), bf16),
            pltpu.VMEM((PLANES * Y, 2, sources, width), bf16),
            sem((3,)),
            sem((2, 2, 3)),
            sem((2 * 2 * Y,)),
            sem((2, 2)),
            sem((2 * Y,)),
            sem((3, 5 + 4 * (outer - 1))),
            sem((3 * outer * CORE,)),
            sem((3,)),
            sem((PLANES * Y,)),
            sem((2,)),
            sem((2,)),
            sem((2,)),
            sem((PLANES * Y,)),
            sem((2, outer)),
            sem((PLANES * Y * outer,)),
        ],
        compiler_params=pltpu.CompilerParams(
            collective_id=0, has_side_effects=True, vmem_limit_bytes=67043328),
    )(transmit, reflect, source_amp, source_cell[None], source_slab[None])
    return out[None]


def solution(mesh):
    pair = mesh.shape["slab"] == PLANES and mesh.shape["blk"] % (Y * CORE) == 0
    return jax.shard_map(
        pair_body if pair else body,
        mesh=mesh,
        in_specs=(
            P("slab", "blk", None),
            P("slab", None, "blk", None),
            P("blk", None),
            P("blk"),
            P("blk"),
        ),
        out_specs=P("slab", "blk", None),
        check_vma=False,
    )
```

profile of v0, /device:TPU:0, one launch (start us, length us, event | category | flops | bytes accessed | tf_op | source)
XLA Modules:
  0.0 55.0 jit_solution(6068307982420234428)
XLA Ops:
  0.0 53.3 %shard_map.55 = f32[32,2048]{1,0:T(8,128)} custom-call(bf16[1,64,2048]{2,1,0:T(8,128)(2,1)} %t_hbm.1, bf16[1,2,64,2048]{3,2,1,0:T(8,128)(2,1)} %r_hbm.1, bf16[32,2048]{1,0:T(8,128)(2,1)} %amp_hbm.1, s32[1,32]{1,0:T(1,128)} %bitcast.4, s32[1,32]{1,0:T(1,128)} %bitcast.5), custom_call_target="tpu_custom_call" | custom-call | tf_op jit(solution)/shard_map/pallas_call | solution.py:431
  53.3 1.7 %copy.7 = f32[1,32,2048]{2,1,0:T(8,128)} copy(f32[1,32,2048]{2,1,0:T(8,128)} %bitcast.3) | data formatting | bytes 524288
where the time goes:
time: 55.4 us; the launch traced here: 55 us
  Pallas kernels  53.3 us (96%)
  local copies, waits for them, and re-layouts  1.67 us (3%)
    pallas_call x1, Pallas kernels, pair_body(): pl.pallas_call(functools.partial(pair_kernel, outer), out_shape=jax.Shape...  53.3 us
    unnamed x1, local copies, waits for them, and re-layouts  1.67 us

commit v1 on v0

--- a/solution.py
+++ b/solution.py
@@ -367,6 +367,32 @@
 
     @pl.when(plane == last)
     def _():
+        for m in range(2):
+            for part in range(2):
+                for k in range(3):
+                    piece_send(m, part, k).wait_send()
+        for part in range(2):
+            for k in range(2):
+                left_push(part, k).wait_send()
+
+    @pl.when(plane != last)
+    def _():
+        for part in range(2):
+            left_relay(part, y).wait_send()
+
+    x_swap(y).wait_send()
+    base_swap(y, plane * Y + y_peer).wait_send()
+    for k in range(3):
+        coup_copy(k, q).wait_send()
+    for ok, m, k, shift in pending:
+        @pl.when(ok)
+        def _():
+            ref = chunk(m, z + shift, core)
+            remote(ref, ref, z_send.at[m, k], z_recv.at[(m * outer + z + shift) * CORE + core],
+                   dev(plane, z, y, c_peer)).wait_send()
+
+    @pl.when(plane == last)
+    def _():
         whole_ref[:, :, cols(q)] = f_ref[:, y]
         for p, yy in others:
             f_copy(0, y, p * Y + yy).wait_recv()
@@ -390,33 +416,14 @@
     def _():
         for j in range(outer):
             d_copy(1, y, q, j).wait_send()
-        for m in range(2):
-            for part in range(2):
-                for k in range(3):
-                    piece_send(m, part, k).wait_send()
-        for part in range(2):
-            for k in range(2):
-                left_push(part, k).wait_send()
 
     @pl.when(plane != last)
     def _():
         f_copy(1, y, q).wait_send()
-        for part in range(2):
-            left_relay(part, y).wait_send()
 
     for j in range(outer):
         d_copy(0, y_peer, q, j).wait_send()
     f_copy(0, y_peer, q).wait_send()
-    x_swap(y).wait_send()
-    base_swap(y, plane * Y + y_peer).wait_send()
-    for k in range(3):
-        coup_copy(k, q).wait_send()
-    for ok, m, k, shift in pending:
-        @pl.when(ok)
-        def _():
-            ref = chunk(m, z + shift, core)
-            remote(ref, ref, z_send.at[m, k], z_recv.at[(m * outer + z + shift) * CORE + core],
-                   dev(plane, z, y, c_peer)).wait_send()
 
 
 def pair_body(transmit, reflect, source_amp, source_cell, source_slab):
@@ -430,7 +437,7 @@
     sem = pltpu.SemaphoreType.DMA
     out = pl.pallas_call(
         functools.partial(pair_kernel, outer),
-        out_shape=jax.ShapeDtypeStruct((sources, double), jnp.float32),
+        out_shape=pltpu.VMEM((sources, double), jnp.float32),
         in_specs=[hbm] * 5,
         out_specs=pl.BlockSpec(memory_space=pltpu.VMEM),
         scratch_shapes=[
@@ -463,8 +470,9 @@
             sem((PLANES * Y * outer,)),
         ],
         compiler_params=pltpu.CompilerParams(
-            collective_id=0, has_side_effects=True, vmem_limit_bytes=67043328),
-    )(transmit, reflect, source_amp, source_cell[None], source_slab[None])
+            collective_id=0, has_side_effects=True, vmem_limit_bytes=32 << 20),
+    )(*(pltpu.with_memory_space_constraint(a, pltpu.HBM) for a in (
+        transmit, reflect, source_amp, source_cell[None], source_slab[None])))
     return out[None]
 
 

time: 55.4 us -> 53.6 us (0.968)
  local copies, waits for them, and re-layouts: 1.67 us -> 0.71 us
  Pallas kernels: 53.3 us -> 52.5 us
    unnamed x1, local copies, waits for them, and re-layouts: 1.67 us -> 0.71 us
    pallas_call x1, Pallas kernels: 53.3 us -> 52.5 us  [pair_body(): pl.pallas_call(functools.partial(pair_kernel, outer), out_shape=pltpu.VME...]
where the time goes in v1:
time: 53.6 us; the launch traced here: 53.2 us
  Pallas kernels  52.5 us (98%)
  local copies, waits for them, and re-layouts  0.71 us (1%)
    pallas_call x1, Pallas kernels, pair_body(): pl.pallas_call(functools.partial(pair_kernel, outer), out_shape=pltpu.VME...  52.5 us

profile of v1, /device:TPU:0, one launch (start us, length us, event | category | flops | bytes accessed | tf_op | source)
XLA Modules:
  0.0 53.2 jit_solution(7707740371318039328)
XLA Ops:
  0.0 52.5 %shard_map.55 = f32[32,2048]{1,0:T(8,128)S(1)} custom-call(bf16[1,64,2048]{2,1,0:T(8,128)(2,1)} %t_hbm.1, bf16[1,2,64,2048]{3,2,1,0:T(8,128)(2,1)} %r_hbm.1, bf16[32,2048]{1,0:T(8,128)(2,1)} %amp_hbm.1, s32[1,32]{1,0:T(1,128)} %bitcast.4, s32[1,32]{1,0:T(1,128)} %bitcast.5), custom_call_target="tpu_custom_call" | custom-call | tf_op jit(solution)/shard_map/pallas_call | solution.py:438
  52.5 0.7 %copy.7 = f32[1,32,2048]{2,1,0:T(8,128)} copy(f32[1,32,2048]{2,1,0:T(8,128)S(1)} %bitcast.3) | data formatting | bytes 524288

commit v2 on v1

v2 whole, which is shorter than its diff:
```python
import functools

import jax
import jax.numpy as jnp
from jax import lax
from jax.experimental import pallas as pl
from jax.experimental.pallas import tpu as pltpu
from jax.sharding import PartitionSpec as P


def shifted(block, axis, distance):
    devices = range(lax.axis_size(axis))
    route = [(i - distance, i) for i in devices if i - distance in devices]
    return lax.ppermute(block, axis, route)


def transposed(matrix):
    half_width = matrix.shape[0]
    return jnp.concatenate([matrix[:, :half_width].T, matrix[:, half_width:].T], 1)


def complex_rows(left_rows, right_matrix):
    inner_width = right_matrix.shape[0]
    outer_width = right_matrix.shape[1] // 2
    row_count = left_rows.shape[0]
    stacked = jnp.concatenate([left_rows[:, :inner_width], left_rows[:, inner_width:]], 0)
    product = jnp.dot(stacked, right_matrix, preferred_element_type=jnp.float32)
    real_out = product[:row_count, :outer_width] - product[row_count:, outer_width:]
    imag_out = product[:row_count, outer_width:] + product[row_count:, :outer_width]
    return jnp.concatenate([real_out, imag_out], 1)


def body(transmit, reflect, source_amp, source_cell, source_slab):
    trans_local = transmit[0]
    refl_local = reflect[0]
    half_width = source_amp.shape[1] // 2
    refl_second = lax.all_gather(refl_local[1], "blk", axis=0, tiled=True)
    coupling = complex_rows(refl_local[0], refl_second).astype(jnp.bfloat16)
    start_rows = trans_local.astype(jnp.float32)
    piece_rows = lax.all_gather(trans_local, "blk", axis=0, tiled=True)
    piece_count = piece_rows.shape[0]
    real_cols = lax.slice_in_dim(coupling, 0, piece_count, axis=1)
    imag_cols = lax.dynamic_slice_in_dim(coupling, half_width, piece_count, 1)
    left_rows = jnp.concatenate([real_cols, imag_cols], 1)
    joined = (start_rows + complex_rows(left_rows, piece_rows)).astype(jnp.bfloat16)
    slab_matrix = lax.all_gather(joined, "blk", axis=0, tiled=True)
    back_matrix = transposed(slab_matrix)
    cell_index = lax.iota(jnp.int32, half_width)
    offset = (cell_index[None, :] - source_cell[:, None]) % half_width
    inside = offset < half_width // 4
    here = source_slab == lax.axis_index("slab")
    keep = inside & here[:, None]
    keep = jnp.concatenate([keep, keep], 1)
    forcing = jnp.where(keep, source_amp, jnp.zeros_like(source_amp))
    chain_length = lax.axis_size("slab")
    carried = forcing
    for sweep_step in range(chain_length - 1):
        arrived = shifted(carried, "slab", 1)
        carried = (forcing.astype(jnp.float32) + complex_rows(arrived, slab_matrix)).astype(
            jnp.bfloat16
        )
    current = carried.astype(jnp.float32)
    for sweep_step in range(chain_length - 1):
        message = complex_rows(current.astype(jnp.bfloat16), back_matrix).astype(jnp.bfloat16)
        arrived = shifted(message, "slab", -1)
        current = carried.astype(jnp.float32) + arrived.astype(jnp.float32)
    return current[None]


MESH = pl.DeviceIdType.MESH
Y = 2
CORE = 2
PLANES = 2


def pair_kernel(
    outer, t_hbm, r_hbm, amp_hbm, cell_hbm, slab_hbm, out_ref,
    amp_ref, cell_ref, slab_ref, g_ref, left_ref, coup_ref, x_ref, base_ref,
    f_ref, whole_ref, d_ref, far_ref,
    ready, arg_sem, in_send, in_recv, left_send, left_recv, z_send, z_recv, relay_send,
    core_send, core_recv, c_send, c_recv, x_send, x_recv, f_send, f_recv, d_send, d_recv,
):
    plane = lax.axis_index("slab")
    me = lax.axis_index("blk")
    z, y, core = me // (Y * CORE), (me // CORE) % Y, me % CORE
    last = PLANES - 1
    depth = t_hbm.shape[1]
    half = depth // 2
    width = t_hbm.shape[2] // 2
    part_width = width // (PLANES * Y)
    sources = amp_hbm.shape[0]
    y_peer, c_peer, x_peer = 1 - y, 1 - core, 1 - plane
    q = plane * Y + y
    f32, bf16 = jnp.float32, jnp.bfloat16
    others = ((x_peer, y), (plane, y_peer), (x_peer, y_peer))
    order = (y, y_peer)

    def dev(p, zz, yy, cc):
        return (p, (zz * Y + yy) * CORE + cc)

    def cols(quarter, base=0):
        return pl.ds(pl.multiple_of(base + quarter * part_width, part_width), part_width)

    def remote(s, d, ss, rs, to):
        return pltpu.make_async_remote_copy(
            src_ref=s, dst_ref=d, send_sem=ss, recv_sem=rs, device_id=to, device_id_type=MESH)

    def valid(zz):
        return (zz >= 0) & (zz < outer)

    def unit(m, zz, yy):
        return g_ref.at[m].at[:, zz * Y + yy, core]

    def piece(m, part, p, yy):
        s = r_hbm.at[0, 1] if m == 0 else t_hbm.at[0]
        return s.at[:, cols(p * Y + yy, part * width)]

    def slot(m, part):
        return g_ref.at[m, part].at[z * Y + y, core]

    def piece_local(m, part):
        return pltpu.make_async_copy(piece(m, part, last, y), slot(m, part), in_recv.at[m * Y + y])

    def piece_send(m, part, p, yy):
        return remote(piece(m, part, p, yy), slot(m, part), in_send.at[m],
                      in_recv.at[m * Y + y], dev(p, z, yy, core))

    def piece_wait(m, yy):
        pltpu.make_async_copy(unit(m, z, yy), unit(m, z, yy), in_recv.at[m * Y + yy]).wait()

    left_units = [(part, h) for part in range(2) for h in range(2)]

    def left_rows(part, h, yy):
        return left_ref.at[part].at[yy, h * half:(h + 1) * half]

    def left_src(part, h):
        return r_hbm.at[0, 0, h * half:(h + 1) * half, part * width:(part + 1) * width]

    def left_local(part):
        return pltpu.make_async_copy(
            r_hbm.at[0, 0, :, part * width:(part + 1) * width], left_ref.at[part].at[y], left_recv.at[0])

    def left_push(u, part, h, k):
        to = dev(0, z, y, core) if k == 0 else dev(last, z, y_peer, core)
        return remote(left_src(part, h), left_rows(part, h, y), left_send.at[0],
                      left_recv.at[u if k == 0 else len(left_units)], to)

    def left_relay(u, part, h):
        ref = left_rows(part, h, y)
        return remote(ref, ref, left_send.at[0], left_recv.at[len(left_units)], dev(plane, z, y_peer, core))

    args = [pltpu.make_async_copy(a, b, arg_sem.at[i]) for i, (a, b) in enumerate(
        ((amp_hbm, amp_ref), (cell_hbm, cell_ref), (slab_hbm, slab_ref)))]

    barrier = pltpu.get_barrier_semaphore()
    for p, zz, yy, cc in ((plane, z, y, c_peer), (plane, z, y_peer, core), (x_peer, z, y, core),
                          (x_peer, z, y_peer, core)):
        pl.semaphore_signal(barrier, inc=1, device_id=dev(p, zz, yy, cc), device_id_type=MESH)
    for s in (1, 2):
        @pl.when(valid(z + s))
        def _():
            pl.semaphore_signal(barrier, inc=1, device_id=dev(plane, z + s, y, core), device_id_type=MESH)

    @pl.when(plane == last)
    def _():
        for m in range(2):
            for part in range(2):
                piece_local(m, part).start()
        for part in range(2):
            left_local(part).start()

    for copy in args:
        copy.start()
    pl.semaphore_wait(barrier, 4 + jnp.minimum(z, 2))
    for s in (1, 2):
        @pl.when(valid(z - s))
        def _():
            pl.semaphore_signal(ready.at[s - 1], inc=1, device_id=dev(plane, z - s, y, core),
                                device_id_type=MESH)

    @pl.when(plane == last)
    def _():
        for p, yy in ((0, y), (last, y_peer), (0, y_peer)):
            for part in range(2):
                piece_send(0, part, p, yy).start()
        for u, (part, h) in enumerate(left_units):
            for k in range(2):
                left_push(u, part, h, k).start()
        for p, yy in ((0, y), (last, y_peer), (0, y_peer)):
            for part in range(2):
                piece_send(1, part, p, yy).start()

    steps = [s for d in range(1, outer) for s in (d, -d)]
    relays = [(s, -1 if s > 0 else 1) for s in steps if abs(s) >= 2 and any(
        0 <= zz + s < outer and 0 <= zz + (-1 if s > 0 else 1) < outer for zz in range(outer))]

    def z_sem(m, shift, yy):
        return z_recv.at[(m * (outer - 1) + shift % outer - 1) * Y + yy]

    def near(m, i, yy, shifts):
        for s in shifts:
            @pl.when(valid(z + s))
            def _():
                remote(unit(m, z, yy), unit(m, z, yy), z_send.at[m * Y + i], z_sem(m, -s, yy),
                       dev(plane, z + s, y, core)).start()

    def relay(m, i, yy, r):
        s, onward = relays[r]
        return remote(unit(m, z + s, yy), unit(m, z + s, yy), relay_send.at[(m * Y + i) * len(relays) + r],
                      z_sem(m, s - onward, yy), dev(plane, z + onward, y, core))

    def relay_ok(r):
        s, onward = relays[r]
        return valid(z + s) & valid(z + onward)

    def landed(m, i, yy, d):
        for s in (d, -d):
            @pl.when(valid(z + s))
            def _():
                remote(unit(m, z + s, yy), unit(m, z + s, yy), z_send.at[0], z_sem(m, s, yy),
                       dev(plane, z, y, c_peer)).wait_recv()
        for r, (s, onward) in enumerate(relays):
            if abs(s) == d:
                @pl.when(relay_ok(r))
                def _():
                    relay(m, i, yy, r).start()

    def chunk(m, zz, cc):
        return g_ref.at[m].at[:, pl.ds(zz * Y, Y), cc]

    def core_copy(m, zz, cc):
        return remote(chunk(m, zz, cc), chunk(m, zz, cc), core_send.at[m], core_recv.at[m * outer + zz],
                      dev(plane, z, y, c_peer))

    def share(m, d):
        for s in ((d, -d) if d else (0,)):
            @pl.when(valid(z + s))
            def _():
                core_copy(m, z + s, core).start()

    def finish(m):
        for zz in range(outer):
            core_copy(m, zz, c_peer).wait_recv()

    def side(m, part):
        return g_ref[m, part].reshape(width, part_width)

    def complex_rows_here(lhs, m):
        n = lhs.shape[0] // 2
        pr = jnp.dot(lhs, side(m, 0), preferred_element_type=f32)
        pi = jnp.dot(lhs, side(m, 1), preferred_element_type=f32)
        return pr[:n] - pi[n:], pi[:n] + pr[n:]

    everyone = (-2, 2, -1, 1)

    def ready_wait(s):
        @pl.when(valid(z + s))
        def _():
            pl.semaphore_wait(ready.at[s - 1], 1)

    def first_push():
        near(0, 0, y, (-2, -1))
        ready_wait(1)
        near(0, 0, y, (1,))
        ready_wait(2)
        near(0, 0, y, (2,))

    @pl.when(plane == last)
    def _():
        piece_wait(0, y)
        first_push()
        piece_wait(0, y_peer)
        near(0, 1, y_peer, everyone)
        share(0, 0)
        piece_wait(1, y)
        near(1, 0, y, everyone)
        landed(0, 0, y, 2)
        landed(0, 0, y, 1)
        piece_wait(1, y_peer)
        near(1, 1, y_peer, everyone)
        share(1, 0)
        pltpu.make_async_copy(left_ref.at[:, y], left_ref.at[:, y], left_recv.at[0]).wait()

    for copy in args:
        copy.wait()
    eye = (lax.broadcasted_iota(jnp.int32, (sources, sources), 0)
           == lax.broadcasted_iota(jnp.int32, (sources, sources), 1))
    cell = jnp.sum(jnp.where(eye, cell_ref[...], 0), axis=1, keepdims=True)
    slab = jnp.sum(jnp.where(eye, slab_ref[...], 0), axis=1, keepdims=True)
    offset = lax.broadcasted_iota(jnp.int32, (sources, width), 1) - cell
    offset = jnp.where(offset < 0, offset + width, offset)
    inside = offset < width // 4
    for part in range(2):
        amp = amp_ref[:, part * width:(part + 1) * width].astype(f32)
        x_ref[part, y] = jnp.where(inside & (slab == 0), amp, 0.0).astype(bf16)
        base_ref[part, y] = jnp.where(inside & (slab == 1), amp, 0.0).astype(bf16)

    @pl.when(plane != last)
    def _():
        piece_wait(0, y)
        first_push()
        piece_wait(0, y_peer)
        near(0, 1, y_peer, everyone)
        share(0, 0)
        for u, (part, h) in enumerate(left_units):
            ref = left_rows(part, h, y)
            pltpu.make_async_copy(ref, ref, left_recv.at[u]).wait()
            left_relay(u, part, h).start()
            if u == 2:
                landed(0, 0, y, 2)
        landed(0, 0, y, 1)
        piece_wait(1, y)
        near(1, 0, y, everyone)
        piece_wait(1, y_peer)
        near(1, 1, y_peer, everyone)
        share(1, 0)

    far = range(3, outer)
    landed(0, 1, y_peer, 2)
    share(0, 2)
    landed(0, 1, y_peer, 1)
    share(0, 1)
    for d in far:
        landed(0, 0, y, d)
        landed(0, 1, y_peer, d)
        share(0, d)
    ref = left_ref.at[:, y_peer]
    pltpu.make_async_copy(ref, ref, left_recv.at[len(left_units)]).wait()
    finish(0)

    def x_swap(yy):
        ref = x_ref.at[:, yy]
        return remote(ref, ref, x_send.at[0], x_recv.at[0], dev(plane, z, y_peer, core))

    def base_swap(yy, quarter):
        ref = base_ref.at[:, yy, :, cols(quarter)]
        return remote(ref, ref, x_send.at[1], x_recv.at[1], dev(plane, z, y_peer, core))

    def coup_copy(yy, k, quarter):
        p, to_y = others[k]
        ref = coup_ref.at[yy].at[:, cols(quarter)]
        return remote(ref, ref, c_send.at[yy], c_recv.at[yy * len(others) + k], dev(p, z, to_y, core))

    re, im = complex_rows_here(left_ref[...].reshape(2 * Y * depth, width), 0)
    for yy in range(Y):
        coup_ref[yy, 0:depth, cols(q)] = re[yy * depth:(yy + 1) * depth].astype(bf16)
        coup_ref[yy, depth:, cols(q)] = im[yy * depth:(yy + 1) * depth].astype(bf16)
        for k in range(len(others)):
            coup_copy(yy, k, q).start()

    x_swap(y).start()
    base_swap(y, plane * Y + y_peer).start()
    landed(1, 0, y, 2)
    landed(1, 0, y, 1)
    landed(1, 1, y_peer, 2)
    share(1, 2)
    landed(1, 1, y_peer, 1)
    share(1, 1)
    for d in far:
        landed(1, 0, y, d)
        landed(1, 1, y_peer, d)
        share(1, d)
    finish(1)

    for yy in range(Y):
        for k, (p, from_y) in enumerate(others):
            coup_copy(yy, k, p * Y + from_y).wait_recv()
        re, im = complex_rows_here(coup_ref[yy], 1)
        for part, value in ((0, re), (1, im)):
            start = g_ref[1, part, z * Y + yy, core]
            g_ref[2, part, z * Y + yy, core] = (value + start.astype(f32)).astype(bf16)
        near(2, yy, yy, everyone)
    share(2, 0)
    for d in (2, 1, *far):
        for yy in range(Y):
            landed(2, yy, yy, d)
        share(2, d)
    x_swap(y_peer).wait_recv()
    base_swap(y_peer, q).wait_recv()
    finish(2)

    re, im = complex_rows_here(x_ref[...].reshape(2 * Y * sources, width), 2)
    for part, value in ((0, re), (1, im)):
        start = base_ref[part, :, :, cols(q)].astype(f32)
        f_ref[part] = (value.reshape(Y, sources, part_width) + start).astype(bf16)

    lhs = f_ref[...].reshape(2 * Y * sources, part_width)
    n = Y * sources
    tile = Y * CORE * depth

    def d_copy(to, k, yy, j):
        spots = slice(j * tile, (j + 1) * tile)
        return remote(d_ref.at[:, yy, :, spots], far_ref.at[k].at[:, :, spots],
                      d_send.at[to], d_recv.at[k * outer + j], dev(0, z, yy, core))

    def f_copy(to, k, yy, quarter):
        return remote(f_ref.at[:, yy], whole_ref.at[:, :, cols(quarter)], f_send.at[to],
                      f_recv.at[k], dev(last, z, yy, core))

    for j in range(outer):
        spots = slice(j * tile, (j + 1) * tile)
        dims = (((1,), (1,)), ((), ()))
        right = [g_ref[2, part, j * Y:(j + 1) * Y].reshape(tile, part_width) for part in range(2)]
        pr = lax.dot_general(lhs, right[0], dims, preferred_element_type=f32)
        pi = lax.dot_general(lhs, right[1], dims, preferred_element_type=f32)
        d_ref[0, :, :, spots] = (pr[:n] - pi[n:]).astype(bf16).reshape(Y, sources, tile)
        d_ref[1, :, :, spots] = (pi[:n] + pr[n:]).astype(bf16).reshape(Y, sources, tile)

        @pl.when(plane == last)
        def _():
            d_copy(0, 2, y_peer, j).start()
            d_copy(1, 0, y, j).start()

        @pl.when(plane != last)
        def _():
            d_copy(0, 1, y_peer, j).start()

    @pl.when(plane == last)
    def _():
        f_copy(0, 1, y_peer, q).start()

    @pl.when(plane != last)
    def _():
        f_copy(0, 2, y_peer, q).start()
        f_copy(1, 0, y, q).start()

    def sent(ref, sem):
        remote(ref, ref, sem, sem, dev(plane, z, y, c_peer)).wait_send()

    @pl.when(plane == last)
    def _():
        for m in range(2):
            sent(r_hbm.at[0, 0, :, 0:6 * part_width], in_send.at[m])
        sent(left_ref, left_send.at[0])

    @pl.when(plane != last)
    def _():
        sent(left_ref.at[:, 0], left_send.at[0])

    x_swap(y).wait_send()
    base_swap(y, plane * Y + y_peer).wait_send()
    for yy in range(Y):
        sent(coup_ref.at[yy, :, 0:len(others) * part_width], c_send.at[yy])
    count = sum(valid(z + s).astype(jnp.int32) for s in everyone)
    for m in range(3):
        sent(g_ref.at[m, :, :, 0], core_send.at[m])
        for i in range(Y):
            for total in range(1, 5):
                @pl.when(count == total)
                def _():
                    sent(g_ref.at[m, :, 0:total, 0], z_send.at[m * Y + i])
            for r in range(len(relays)):
                @pl.when(relay_ok(r))
                def _():
                    sent(g_ref.at[m, :, 0, 0], relay_send.at[(m * Y + i) * len(relays) + r])

    @pl.when(plane == last)
    def _():
        whole_ref[:, :, cols(q)] = f_ref[:, y]
        for k, (p, yy) in enumerate(others):
            f_copy(0, k, y, p * Y + yy).wait_recv()
        for part in range(2):
            out_ref[:, part * width:(part + 1) * width] = whole_ref[part].astype(f32)
        sent(d_ref.at[:, 0], d_send.at[0])
        sent(d_ref.at[:, 0], d_send.at[1])
        sent(f_ref.at[:, 0], f_send.at[0])

    @pl.when(plane != last)
    def _():
        for j in range(outer):
            spots = slice(j * tile, (j + 1) * tile)
            for k in range(len(others)):
                d_copy(0, k, y, j).wait_recv()
            for part in range(2):
                total = d_ref.at[part][y, :, spots].astype(f32)
                for k in range(len(others)):
                    total = total + far_ref[k, part, :, spots].astype(f32)
                out_ref[:, part * width + j * tile:part * width + (j + 1) * tile] = (
                    x_ref.at[part][y, :, spots].astype(f32) + total.astype(bf16).astype(f32))
        sent(d_ref.at[:, 0], d_send.at[0])
        sent(f_ref.at[:, 0], f_send.at[0])
        sent(f_ref.at[:, 0], f_send.at[1])


def pair_body(transmit, reflect, source_amp, source_cell, source_slab):
    outer = lax.axis_size("blk") // (Y * CORE)
    sources, double = source_amp.shape
    depth = transmit.shape[1]
    width = double // 2
    quarter = width // (PLANES * Y)
    bf16 = jnp.bfloat16
    hbm = pl.BlockSpec(memory_space=pltpu.HBM)
    sem = pltpu.SemaphoreType.DMA
    out = pl.pallas_call(
        functools.partial(pair_kernel, outer),
        out_shape=pltpu.VMEM((sources, double), jnp.float32),
        in_specs=[hbm] * 5,
        out_specs=pl.BlockSpec(memory_space=pltpu.VMEM),
        scratch_shapes=[
            pltpu.VMEM((sources, double), bf16),
            pltpu.VMEM((1, sources), jnp.int32),
            pltpu.VMEM((1, sources), jnp.int32),
            pltpu.VMEM((3, 2, outer * Y, CORE, depth, quarter), bf16),
            pltpu.VMEM((2, Y, depth, width), bf16),
            pltpu.VMEM((Y, 2 * depth, width), bf16),
            pltpu.VMEM((2, Y, sources, width), bf16),
            pltpu.VMEM((2, Y, sources, width), bf16),
            pltpu.VMEM((2, Y, sources, quarter), bf16),
            pltpu.VMEM((2, sources, width), bf16),
            pltpu.VMEM((2, Y, sources, width), bf16),
            pltpu.VMEM((PLANES * Y - 1, 2, sources, width), bf16),
            pltpu.SemaphoreType.REGULAR((2,)),
            sem((3,)),
            sem((2,)),
            sem((2 * Y,)),
            sem((1,)),
            sem((5,)),
            sem((3 * Y,)),
            sem((3 * (outer - 1) * Y,)),
            sem((3 * Y * 2 * max(outer - 3, 1),)),
            sem((3,)),
            sem((3 * outer,)),
            sem((Y,)),
            sem((3 * Y,)),
            sem((2,)),
            sem((2,)),
            sem((2,)),
            sem((3,)),
            sem((2,)),
            sem((3 * outer,)),
        ],
        compiler_params=pltpu.CompilerParams(
            collective_id=0, has_side_effects=True, vmem_limit_bytes=32 << 20),
    )(*(pltpu.with_memory_space_constraint(a, pltpu.HBM) for a in (
        transmit, reflect, source_amp, source_cell[None], source_slab[None])))
    return out[None]


def solution(mesh):
    pair = mesh.shape["slab"] == PLANES and mesh.shape["blk"] % (Y * CORE) == 0
    return jax.shard_map(
        pair_body if pair else body,
        mesh=mesh,
        in_specs=(
            P("slab", "blk", None),
            P("slab", None, "blk", None),
            P("blk", None),
            P("blk"),
            P("blk"),
        ),
        out_specs=P("slab", "blk", None),
        check_vma=False,
    )
```

time: 53.6 us -> 52.9 us (0.987)
  no operation moved by 1% of the time
where the time goes in v2:
time: 52.9 us; the launch traced here: 52.7 us
  Pallas kernels  52 us (98%)
  local copies, waits for them, and re-layouts  0.71 us (1%)
    pallas_call x1, Pallas kernels, pair_body(): pl.pallas_call(functools.partial(pair_kernel, outer), out_shape=pltpu.VME...  52 us

profile of v2, /device:TPU:0, one launch (start us, length us, event | category | flops | bytes accessed | tf_op | source)
XLA Modules:
  0.0 52.7 jit_solution(1955033555161201888)
XLA Ops:
  0.0 52.0 %shard_map.55 = f32[32,2048]{1,0:T(8,128)S(1)} custom-call(bf16[1,64,2048]{2,1,0:T(8,128)(2,1)} %t_hbm.1, bf16[1,2,64,2048]{3,2,1,0:T(8,128)(2,1)} %r_hbm.1, bf16[32,2048]{1,0:T(8,128)(2,1)} %amp_hbm.1, s32[1,32]{1,0:T(1,128)} %bitcast.4, s32[1,32]{1,0:T(1,128)} %bitcast.5), custom_call_target="tpu_custom_call" | custom-call | tf_op jit(solution)/shard_map/pallas_call | solution.py:494
  52.0 0.7 %copy.7 = f32[1,32,2048]{2,1,0:T(8,128)} copy(f32[1,32,2048]{2,1,0:T(8,128)S(1)} %bitcast.3) | data formatting | bytes 524288

commit v3 on v2

--- a/solution.py
+++ b/solution.py
@@ -197,9 +197,13 @@
     def z_sem(m, shift, yy):
         return z_recv.at[(m * (outer - 1) + shift % outer - 1) * Y + yy]
 
-    def near(m, i, yy, shifts):
+    def relays_to(s):
+        return functools.reduce(jnp.logical_or, [relay_ok(r) for r in range(len(relays)) if relays[r][1] == s],
+                                jnp.logical_and(z < 0, z > 0))
+
+    def near(m, i, yy, shifts, when=lambda s: True):
         for s in shifts:
-            @pl.when(valid(z + s))
+            @pl.when(valid(z + s) & when(s))
             def _():
                 remote(unit(m, z, yy), unit(m, z, yy), z_send.at[m * Y + i], z_sem(m, -s, yy),
                        dev(plane, z + s, y, core)).start()
@@ -273,12 +277,15 @@
         near(0, 1, y_peer, everyone)
         share(0, 0)
         piece_wait(1, y)
-        near(1, 0, y, everyone)
+        near(1, 0, y, everyone, lambda s: ~relays_to(s))
         landed(0, 0, y, 2)
         landed(0, 0, y, 1)
         piece_wait(1, y_peer)
-        near(1, 1, y_peer, everyone)
+        near(1, 1, y_peer, everyone, lambda s: ~relays_to(s))
         share(1, 0)
+        landed(0, 1, y_peer, 2)
+        near(1, 0, y, (-1, 1), relays_to)
+        near(1, 1, y_peer, (-1, 1), relays_to)
         pltpu.make_async_copy(left_ref.at[:, y], left_ref.at[:, y], left_recv.at[0]).wait()
 
     for copy in args:
@@ -309,6 +316,7 @@
             if u == 2:
                 landed(0, 0, y, 2)
         landed(0, 0, y, 1)
+        landed(0, 1, y_peer, 2)
         piece_wait(1, y)
         near(1, 0, y, everyone)
         piece_wait(1, y_peer)
@@ -316,7 +324,6 @@
         share(1, 0)
 
     far = range(3, outer)
-    landed(0, 1, y_peer, 2)
     share(0, 2)
     landed(0, 1, y_peer, 1)
     share(0, 1)

time: 52.9 us -> 49.3 us (0.932)
  Pallas kernels: 52 us -> 48.5 us
    pallas_call x1, Pallas kernels: 52 us -> 48.5 us  [pair_body(): pl.pallas_call(functools.partial(pair_kernel, outer), out_shape=pltpu.VME...]
where the time goes in v3:
time: 49.3 us; the launch traced here: 49.2 us
  Pallas kernels  48.5 us (98%)
  local copies, waits for them, and re-layouts  0.71 us (1%)
    pallas_call x1, Pallas kernels, pair_body(): pl.pallas_call(functools.partial(pair_kernel, outer), out_shape=pltpu.VME...  48.5 us

profile of v3, /device:TPU:0, one launch (start us, length us, event | category | flops | bytes accessed | tf_op | source)
XLA Modules:
  0.0 49.2 jit_solution(4034837816258170307)
XLA Ops:
  0.0 48.5 %shard_map.55 = f32[32,2048]{1,0:T(8,128)S(1)} custom-call(bf16[1,64,2048]{2,1,0:T(8,128)(2,1)} %t_hbm.1, bf16[1,2,64,2048]{3,2,1,0:T(8,128)(2,1)} %r_hbm.1, bf16[32,2048]{1,0:T(8,128)(2,1)} %amp_hbm.1, s32[1,32]{1,0:T(1,128)} %bitcast.4, s32[1,32]{1,0:T(1,128)} %bitcast.5), custom_call_target="tpu_custom_call" | custom-call | tf_op jit(solution)/shard_map/pallas_call | solution.py:501
  48.5 0.7 %copy.7 = f32[1,32,2048]{2,1,0:T(8,128)} copy(f32[1,32,2048]{2,1,0:T(8,128)S(1)} %bitcast.3) | data formatting | bytes 524288

commit v4 on v2

--- a/solution.py
+++ b/solution.py
@@ -105,6 +105,12 @@
         return pltpu.make_async_remote_copy(
             src_ref=s, dst_ref=d, send_sem=ss, recv_sem=rs, device_id=to, device_id_type=MESH)
 
+    def got(ref, sem):
+        pltpu.make_async_copy(ref, ref, sem).wait()
+
+    def sent(ref, sem):
+        remote(ref, ref, sem, sem, dev(plane, z, y, c_peer)).wait_send()
+
     def valid(zz):
         return (zz >= 0) & (zz < outer)
 
@@ -122,11 +128,12 @@
         return pltpu.make_async_copy(piece(m, part, last, y), slot(m, part), in_recv.at[m * Y + y])
 
     def piece_send(m, part, p, yy):
-        return remote(piece(m, part, p, yy), slot(m, part), in_send.at[m],
-                      in_recv.at[m * Y + y], dev(p, z, yy, core))
+        split = m == 0 and part == 1 and p != last and yy is y
+        return remote(piece(m, part, p, yy), slot(m, part), in_send.at[0],
+                      in_recv.at[2 * Y] if split else in_recv.at[m * Y + y], dev(p, z, yy, core))
 
     def piece_wait(m, yy):
-        pltpu.make_async_copy(unit(m, z, yy), unit(m, z, yy), in_recv.at[m * Y + yy]).wait()
+        got(unit(m, z, yy), in_recv.at[m * Y + yy])
 
     left_units = [(part, h) for part in range(2) for h in range(2)]
 
@@ -153,13 +160,16 @@
         ((amp_hbm, amp_ref), (cell_hbm, cell_ref), (slab_hbm, slab_ref)))]
 
     barrier = pltpu.get_barrier_semaphore()
-    for p, zz, yy, cc in ((plane, z, y, c_peer), (plane, z, y_peer, core), (x_peer, z, y, core),
-                          (x_peer, z, y_peer, core)):
-        pl.semaphore_signal(barrier, inc=1, device_id=dev(p, zz, yy, cc), device_id_type=MESH)
+
+    def tell(sem, to, when=None):
+        def send():
+            pl.semaphore_signal(sem, inc=1, device_id=to, device_id_type=MESH)
+        send() if when is None else pl.when(when)(send)
+
+    for p, yy, cc in ((plane, y, c_peer), (plane, y_peer, core), (x_peer, y, core), (x_peer, y_peer, core)):
+        tell(barrier, dev(p, z, yy, cc))
     for s in (1, 2):
-        @pl.when(valid(z + s))
-        def _():
-            pl.semaphore_signal(barrier, inc=1, device_id=dev(plane, z + s, y, core), device_id_type=MESH)
+        tell(barrier, dev(plane, z + s, y, core), valid(z + s))
 
     @pl.when(plane == last)
     def _():
@@ -173,10 +183,7 @@
         copy.start()
     pl.semaphore_wait(barrier, 4 + jnp.minimum(z, 2))
     for s in (1, 2):
-        @pl.when(valid(z - s))
-        def _():
-            pl.semaphore_signal(ready.at[s - 1], inc=1, device_id=dev(plane, z - s, y, core),
-                                device_id_type=MESH)
+        tell(ready.at[s - 1], dev(plane, z - s, y, core), valid(z - s))
 
     @pl.when(plane == last)
     def _():
@@ -190,46 +197,51 @@
             for part in range(2):
                 piece_send(1, part, p, yy).start()
 
-    steps = [s for d in range(1, outer) for s in (d, -d)]
-    relays = [(s, -1 if s > 0 else 1) for s in steps if abs(s) >= 2 and any(
-        0 <= zz + s < outer and 0 <= zz + (-1 if s > 0 else 1) < outer for zz in range(outer))]
-
     def z_sem(m, shift, yy):
         return z_recv.at[(m * (outer - 1) + shift % outer - 1) * Y + yy]
 
-    def near(m, i, yy, shifts):
+    reach = (-2, 2, -1, 1)
+
+    def near(m, yy, when=lambda s: True, part=None, shifts=reach):
         for s in shifts:
-            @pl.when(valid(z + s))
+            @pl.when(valid(z + s) & when(s))
             def _():
-                remote(unit(m, z, yy), unit(m, z, yy), z_send.at[m * Y + i], z_sem(m, -s, yy),
-                       dev(plane, z + s, y, core)).start()
-
-    def relay(m, i, yy, r):
-        s, onward = relays[r]
-        return remote(unit(m, z + s, yy), unit(m, z + s, yy), relay_send.at[(m * Y + i) * len(relays) + r],
-                      z_sem(m, s - onward, yy), dev(plane, z + onward, y, core))
-
-    def relay_ok(r):
-        s, onward = relays[r]
-        return valid(z + s) & valid(z + onward)
-
-    def landed(m, i, yy, d):
+                ref = unit(m, z, yy) if part is None else slot(m, part)
+                remote(ref, ref, z_send.at[0], z_sem(m, -s, yy), dev(plane, z + s, y, core)).start()
+
+    def ready_wait(s):
+        @pl.when(valid(z + s))
+        def _():
+            pl.semaphore_wait(ready.at[s - 1], 1)
+
+    def relays_to(s):
+        return {1: (z >= 2) & valid(z + 1), -1: (z <= outer - 3) & valid(z - 1)}.get(s, z < 0)
+
+    def onward_ok(s):
+        return valid(z + s) & valid(z + (-1 if s > 0 else 1)) & (abs(s) > 1)
+
+    def hop(m, yy, d):
+        for s in (d, -d) if d > 1 else ():
+            @pl.when(onward_ok(s))
+            def _():
+                onward = -1 if s > 0 else 1
+                ref = unit(m, z + s, yy)
+                got(ref, z_sem(m, s, yy))
+                remote(ref, ref, relay_send.at[0], z_sem(m, s - onward, yy),
+                       dev(plane, z + onward, y, core)).start()
+
+    def rest(m, d):
         for s in (d, -d):
-            @pl.when(valid(z + s))
+            @pl.when(valid(z + s) & ~onward_ok(s))
             def _():
-                remote(unit(m, z + s, yy), unit(m, z + s, yy), z_send.at[0], z_sem(m, s, yy),
-                       dev(plane, z, y, c_peer)).wait_recv()
-        for r, (s, onward) in enumerate(relays):
-            if abs(s) == d:
-                @pl.when(relay_ok(r))
-                def _():
-                    relay(m, i, yy, r).start()
+                for yy in range(Y):
+                    got(unit(m, z + s, yy), z_sem(m, s, yy))
 
     def chunk(m, zz, cc):
         return g_ref.at[m].at[:, pl.ds(zz * Y, Y), cc]
 
     def core_copy(m, zz, cc):
-        return remote(chunk(m, zz, cc), chunk(m, zz, cc), core_send.at[m], core_recv.at[m * outer + zz],
+        return remote(chunk(m, zz, cc), chunk(m, zz, cc), core_send.at[0], core_recv.at[m],
                       dev(plane, z, y, c_peer))
 
     def share(m, d):
@@ -239,8 +251,13 @@
                 core_copy(m, z + s, core).start()
 
     def finish(m):
-        for zz in range(outer):
-            core_copy(m, zz, c_peer).wait_recv()
+        got(g_ref.at[m].at[:, :, c_peer], core_recv.at[m])
+
+    def collect(m):
+        for d in range(1, outer):
+            rest(m, d)
+            share(m, d)
+        finish(m)
 
     def side(m, part):
         return g_ref[m, part].reshape(width, part_width)
@@ -251,35 +268,29 @@
         pi = jnp.dot(lhs, side(m, 1), preferred_element_type=f32)
         return pr[:n] - pi[n:], pi[:n] + pr[n:]
 
-    everyone = (-2, 2, -1, 1)
-
-    def ready_wait(s):
-        @pl.when(valid(z + s))
-        def _():
-            pl.semaphore_wait(ready.at[s - 1], 1)
-
-    def first_push():
-        near(0, 0, y, (-2, -1))
+    @pl.when(plane == last)
+    def _():
+        piece_wait(0, y)
+        near(0, y, shifts=(-2, -1))
         ready_wait(1)
-        near(0, 0, y, (1,))
+        near(0, y, shifts=(1,))
         ready_wait(2)
-        near(0, 0, y, (2,))
-
-    @pl.when(plane == last)
-    def _():
-        piece_wait(0, y)
-        first_push()
+        near(0, y, shifts=(2,))
         piece_wait(0, y_peer)
-        near(0, 1, y_peer, everyone)
+        near(0, y_peer)
         share(0, 0)
         piece_wait(1, y)
-        near(1, 0, y, everyone)
-        landed(0, 0, y, 2)
-        landed(0, 0, y, 1)
+        near(1, y, lambda s: ~relays_to(s))
+        hop(0, y, 2)
+        hop(0, y_peer, 2)
+        for yy in order:
+            for d in range(3, outer):
+                hop(0, yy, d)
+        near(1, y, relays_to)
         piece_wait(1, y_peer)
-        near(1, 1, y_peer, everyone)
+        near(1, y_peer)
         share(1, 0)
-        pltpu.make_async_copy(left_ref.at[:, y], left_ref.at[:, y], left_recv.at[0]).wait()
+        got(left_ref.at[:, y], left_recv.at[0])
 
     for copy in args:
         copy.wait()
@@ -297,35 +308,31 @@
 
     @pl.when(plane != last)
     def _():
-        piece_wait(0, y)
-        first_push()
+        ready_wait(1)
+        ready_wait(2)
+        for part in range(2):
+            got(slot(0, part), in_recv.at[y] if part == 0 else in_recv.at[2 * Y])
+            near(0, y, part=part)
         piece_wait(0, y_peer)
-        near(0, 1, y_peer, everyone)
+        near(0, y_peer)
         share(0, 0)
+        hops = [(y, 1), (y, 2), (y_peer, 1), (y_peer, 2)]
         for u, (part, h) in enumerate(left_units):
-            ref = left_rows(part, h, y)
-            pltpu.make_async_copy(ref, ref, left_recv.at[u]).wait()
+            got(left_rows(part, h, y), left_recv.at[u])
             left_relay(u, part, h).start()
-            if u == 2:
-                landed(0, 0, y, 2)
-        landed(0, 0, y, 1)
-        piece_wait(1, y)
-        near(1, 0, y, everyone)
-        piece_wait(1, y_peer)
-        near(1, 1, y_peer, everyone)
+            hop(0, *hops[u])
+        for yy in order:
+            for d in range(3, outer):
+                hop(0, yy, d)
+        for yy in order:
+            piece_wait(1, yy)
+            near(1, yy)
         share(1, 0)
 
-    far = range(3, outer)
-    landed(0, 1, y_peer, 2)
-    share(0, 2)
-    landed(0, 1, y_peer, 1)
-    share(0, 1)
-    for d in far:
-        landed(0, 0, y, d)
-        landed(0, 1, y_peer, d)
+    for d in range(1, outer):
+        rest(0, d)
         share(0, d)
-    ref = left_ref.at[:, y_peer]
-    pltpu.make_async_copy(ref, ref, left_recv.at[len(left_units)]).wait()
+    got(left_ref.at[:, y_peer], left_recv.at[len(left_units)])
     finish(0)
 
     def x_swap(yy):
@@ -339,7 +346,7 @@
     def coup_copy(yy, k, quarter):
         p, to_y = others[k]
         ref = coup_ref.at[yy].at[:, cols(quarter)]
-        return remote(ref, ref, c_send.at[yy], c_recv.at[yy * len(others) + k], dev(p, z, to_y, core))
+        return remote(ref, ref, c_send.at[0], c_recv.at[yy], dev(p, z, to_y, core))
 
     re, im = complex_rows_here(left_ref[...].reshape(2 * Y * depth, width), 0)
     for yy in range(Y):
@@ -350,30 +357,25 @@
 
     x_swap(y).start()
     base_swap(y, plane * Y + y_peer).start()
-    landed(1, 0, y, 2)
-    landed(1, 0, y, 1)
-    landed(1, 1, y_peer, 2)
-    share(1, 2)
-    landed(1, 1, y_peer, 1)
-    share(1, 1)
-    for d in far:
-        landed(1, 0, y, d)
-        landed(1, 1, y_peer, d)
-        share(1, d)
-    finish(1)
-
+
+    for yy in order:
+        for d in range(2, outer):
+            hop(1, yy, d)
+    collect(1)
+    trio = len(others) * part_width
     for yy in range(Y):
-        for k, (p, from_y) in enumerate(others):
-            coup_copy(yy, k, p * Y + from_y).wait_recv()
+        got(coup_ref.at[yy, :, 0:trio], c_recv.at[yy])
         re, im = complex_rows_here(coup_ref[yy], 1)
         for part, value in ((0, re), (1, im)):
             start = g_ref[1, part, z * Y + yy, core]
             g_ref[2, part, z * Y + yy, core] = (value + start.astype(f32)).astype(bf16)
-        near(2, yy, yy, everyone)
+        near(2, yy)
     share(2, 0)
-    for d in (2, 1, *far):
+    for d in range(1, outer):
         for yy in range(Y):
-            landed(2, yy, yy, d)
+            hop(2, yy, d)
+    for d in range(1, outer):
+        rest(2, d)
         share(2, d)
     x_swap(y_peer).wait_recv()
     base_swap(y_peer, q).wait_recv()
@@ -388,14 +390,14 @@
     n = Y * sources
     tile = Y * CORE * depth
 
-    def d_copy(to, k, yy, j):
+    def d_copy(k, yy, j):
         spots = slice(j * tile, (j + 1) * tile)
         return remote(d_ref.at[:, yy, :, spots], far_ref.at[k].at[:, :, spots],
-                      d_send.at[to], d_recv.at[k * outer + j], dev(0, z, yy, core))
-
-    def f_copy(to, k, yy, quarter):
-        return remote(f_ref.at[:, yy], whole_ref.at[:, :, cols(quarter)], f_send.at[to],
-                      f_recv.at[k], dev(last, z, yy, core))
+                      d_send.at[0], d_recv.at[j], dev(0, z, yy, core))
+
+    def f_copy(yy):
+        return remote(f_ref.at[:, yy], whole_ref.at[:, :, cols(q)], f_send.at[0],
+                      f_recv.at[0], dev(last, z, yy, core))
 
     for j in range(outer):
         spots = slice(j * tile, (j + 1) * tile)
@@ -408,29 +410,25 @@
 
         @pl.when(plane == last)
         def _():
-            d_copy(0, 2, y_peer, j).start()
-            d_copy(1, 0, y, j).start()
+            d_copy(2, y_peer, j).start()
+            d_copy(0, y, j).start()
 
         @pl.when(plane != last)
         def _():
-            d_copy(0, 1, y_peer, j).start()
+            d_copy(1, y_peer, j).start()
 
     @pl.when(plane == last)
     def _():
-        f_copy(0, 1, y_peer, q).start()
+        f_copy(y_peer).start()
 
     @pl.when(plane != last)
     def _():
-        f_copy(0, 2, y_peer, q).start()
-        f_copy(1, 0, y, q).start()
-
-    def sent(ref, sem):
-        remote(ref, ref, sem, sem, dev(plane, z, y, c_peer)).wait_send()
+        f_copy(y_peer).start()
+        f_copy(y).start()
 
     @pl.when(plane == last)
     def _():
-        for m in range(2):
-            sent(r_hbm.at[0, 0, :, 0:6 * part_width], in_send.at[m])
+        sent(r_hbm.at[0, :, :, 0:6 * part_width], in_send.at[0])
         sent(left_ref, left_send.at[0])
 
     @pl.when(plane != last)
@@ -439,38 +437,32 @@
 
     x_swap(y).wait_send()
     base_swap(y, plane * Y + y_peer).wait_send()
-    for yy in range(Y):
-        sent(coup_ref.at[yy, :, 0:len(others) * part_width], c_send.at[yy])
-    count = sum(valid(z + s).astype(jnp.int32) for s in everyone)
-    for m in range(3):
-        sent(g_ref.at[m, :, :, 0], core_send.at[m])
-        for i in range(Y):
-            for total in range(1, 5):
-                @pl.when(count == total)
-                def _():
-                    sent(g_ref.at[m, :, 0:total, 0], z_send.at[m * Y + i])
-            for r in range(len(relays)):
-                @pl.when(relay_ok(r))
-                def _():
-                    sent(g_ref.at[m, :, 0, 0], relay_send.at[(m * Y + i) * len(relays) + r])
+    sent(coup_ref.at[:, :, 0:trio], c_send.at[0])
+    sent(g_ref.at[:, :, :, 0], core_send.at[0])
+    for zz in range(outer):
+        count = sum(0 <= zz + s < outer for s in reach)
+        hops = (max(zz - 1, 0) + max(outer - 2 - zz, 0)) * (0 < zz < outer - 1)
+
+        @pl.when(z == zz)
+        def _():
+            sent(g_ref.at[:, :, 0:Y * count, 0], z_send.at[0])
+            if hops:
+                sent(g_ref.at[:, :, 0:Y * hops, 0], relay_send.at[0])
 
     @pl.when(plane == last)
     def _():
         whole_ref[:, :, cols(q)] = f_ref[:, y]
-        for k, (p, yy) in enumerate(others):
-            f_copy(0, k, y, p * Y + yy).wait_recv()
+        got(whole_ref.at[:, :, 0:trio], f_recv.at[0])
         for part in range(2):
             out_ref[:, part * width:(part + 1) * width] = whole_ref[part].astype(f32)
-        sent(d_ref.at[:, 0], d_send.at[0])
-        sent(d_ref.at[:, 0], d_send.at[1])
+        sent(d_ref, d_send.at[0])
         sent(f_ref.at[:, 0], f_send.at[0])
 
     @pl.when(plane != last)
     def _():
         for j in range(outer):
             spots = slice(j * tile, (j + 1) * tile)
-            for k in range(len(others)):
-                d_copy(0, k, y, j).wait_recv()
+            got(far_ref.at[:, :, :, spots], d_recv.at[j])
             for part in range(2):
                 total = d_ref.at[part][y, :, spots].astype(f32)
                 for k in range(len(others)):
@@ -478,8 +470,7 @@
                 out_ref[:, part * width + j * tile:part * width + (j + 1) * tile] = (
                     x_ref.at[part][y, :, spots].astype(f32) + total.astype(bf16).astype(f32))
         sent(d_ref.at[:, 0], d_send.at[0])
-        sent(f_ref.at[:, 0], f_send.at[0])
-        sent(f_ref.at[:, 0], f_send.at[1])
+        sent(f_ref, f_send.at[0])
 
 
 def pair_body(transmit, reflect, source_amp, source_cell, source_slab):
@@ -511,23 +502,23 @@
             pltpu.VMEM((PLANES * Y - 1, 2, sources, width), bf16),
             pltpu.SemaphoreType.REGULAR((2,)),
             sem((3,)),
-            sem((2,)),
-            sem((2 * Y,)),
+            sem((1,)),
+            sem((2 * Y + 1,)),
             sem((1,)),
             sem((5,)),
-            sem((3 * Y,)),
+            sem((1,)),
             sem((3 * (outer - 1) * Y,)),
-            sem((3 * Y * 2 * max(outer - 3, 1),)),
+            sem((1,)),
+            sem((1,)),
             sem((3,)),
-            sem((3 * outer,)),
+            sem((1,)),
             sem((Y,)),
-            sem((3 * Y,)),
             sem((2,)),
             sem((2,)),
-            sem((2,)),
-            sem((3,)),
-            sem((2,)),
-            sem((3 * outer,)),
+            sem((1,)),
+            sem((1,)),
+            sem((1,)),
+            sem((outer,)),
         ],
         compiler_params=pltpu.CompilerParams(
             collective_id=0, has_side_effects=True, vmem_limit_bytes=32 << 20),
@@ -537,7 +528,7 @@
 
 
 def solution(mesh):
-    pair = mesh.shape["slab"] == PLANES and mesh.shape["blk"] % (Y * CORE) == 0
+    pair = mesh.shape["slab"] == PLANES and mesh.shape["blk"] % (Y * CORE) == 0 and mesh.shape["blk"] > 2 * Y * CORE
     return jax.shard_map(
         pair_body if pair else body,
         mesh=mesh,

time: 52.9 us -> 47.8 us (0.904)
  Pallas kernels: 52 us -> 46.9 us
    pallas_call x1, Pallas kernels: 52 us -> 46.9 us  [pair_body(): pl.pallas_call(functools.partial(pair_kernel, outer), out_shape=pltpu.VME...]
where the time goes in v4:
time: 47.8 us; the launch traced here: 47.6 us
  Pallas kernels  46.9 us (98%)
  local copies, waits for them, and re-layouts  0.71 us (1%)
    pallas_call x1, Pallas kernels, pair_body(): pl.pallas_call(functools.partial(pair_kernel, outer), out_shape=pltpu.VME...  46.9 us

profile of v4, /device:TPU:0, one launch (start us, length us, event | category | flops | bytes accessed | tf_op | source)
XLA Modules:
  0.0 47.6 jit_solution(9578295087315405160)
XLA Ops:
  0.0 46.9 %shard_map.55 = f32[32,2048]{1,0:T(8,128)S(1)} custom-call(bf16[1,64,2048]{2,1,0:T(8,128)(2,1)} %t_hbm.1, bf16[1,2,64,2048]{3,2,1,0:T(8,128)(2,1)} %r_hbm.1, bf16[32,2048]{1,0:T(8,128)(2,1)} %amp_hbm.1, s32[1,32]{1,0:T(1,128)} %bitcast.4, s32[1,32]{1,0:T(1,128)} %bitcast.5), custom_call_target="tpu_custom_call" | custom-call | tf_op jit(solution)/shard_map/pallas_call | solution.py:485
  46.9 0.7 %copy.7 = f32[1,32,2048]{2,1,0:T(8,128)} copy(f32[1,32,2048]{2,1,0:T(8,128)S(1)} %bitcast.3) | data formatting | bytes 524288

commit v5 on v4

--- a/solution.py
+++ b/solution.py
@@ -71,14 +71,15 @@
 Y = 2
 CORE = 2
 PLANES = 2
+SPLIT = 4
 
 
 def pair_kernel(
     outer, t_hbm, r_hbm, amp_hbm, cell_hbm, slab_hbm, out_ref,
     amp_ref, cell_ref, slab_ref, g_ref, left_ref, coup_ref, x_ref, base_ref,
-    f_ref, whole_ref, d_ref, far_ref,
+    f_ref, whole_ref, d_ref, far_ref, hand_ref,
     ready, arg_sem, in_send, in_recv, left_send, left_recv, z_send, z_recv, relay_send,
-    core_send, core_recv, c_send, c_recv, x_send, x_recv, f_send, f_recv, d_send, d_recv,
+    core_send, core_recv, c_send, c_recv, x_send, x_recv, f_send, f_recv, d_send, d_recv, hand_recv,
 ):
     plane = lax.axis_index("slab")
     me = lax.axis_index("blk")
@@ -94,6 +95,9 @@
     f32, bf16 = jnp.float32, jnp.bfloat16
     others = ((x_peer, y), (plane, y_peer), (x_peer, y_peer))
     order = (y, y_peer)
+    rows = coup_ref.shape[1] // 2
+    per = depth // rows
+    parts = range(Y * per)
 
     def dev(p, zz, yy, cc):
         return (p, (zz * Y + yy) * CORE + cc)
@@ -114,8 +118,10 @@
     def valid(zz):
         return (zz >= 0) & (zz < outer)
 
-    def unit(m, zz, yy):
-        return g_ref.at[m].at[:, zz * Y + yy, core]
+    def unit(m, zz, u):
+        if m < 2:
+            return g_ref.at[m].at[:, zz * Y + u, core]
+        return g_ref.at[m].at[:, zz * Y + u // per, core, u % per * rows:(u % per + 1) * rows]
 
     def piece(m, part, p, yy):
         s = r_hbm.at[0, 1] if m == 0 else t_hbm.at[0]
@@ -198,7 +204,8 @@
                 piece_send(1, part, p, yy).start()
 
     def z_sem(m, shift, yy):
-        return z_recv.at[(m * (outer - 1) + shift % outer - 1) * Y + yy]
+        k = shift % outer - 1
+        return z_recv.at[(m * (outer - 1) + k) * Y + yy if m < 2 else (2 * (outer - 1) + k * per) * Y + yy]
 
     reach = (-2, 2, -1, 1)
 
@@ -208,6 +215,12 @@
             def _():
                 ref = unit(m, z, yy) if part is None else slot(m, part)
                 remote(ref, ref, z_send.at[0], z_sem(m, -s, yy), dev(plane, z + s, y, core)).start()
+
+    def inner(s):
+        return (z + s > 0) & (z + s < outer - 1) if abs(s) == 1 else z < 0
+
+    def outward(s):
+        return ~inner(s)
 
     def ready_wait(s):
         @pl.when(valid(z + s))
@@ -234,7 +247,7 @@
         for s in (d, -d):
             @pl.when(valid(z + s) & ~onward_ok(s))
             def _():
-                for yy in range(Y):
+                for yy in range(Y) if m < 2 else parts:
                     got(unit(m, z + s, yy), z_sem(m, s, yy))
 
     def chunk(m, zz, cc):
@@ -349,11 +362,11 @@
         return remote(ref, ref, c_send.at[0], c_recv.at[yy], dev(p, z, to_y, core))
 
     re, im = complex_rows_here(left_ref[...].reshape(2 * Y * depth, width), 0)
-    for yy in range(Y):
-        coup_ref[yy, 0:depth, cols(q)] = re[yy * depth:(yy + 1) * depth].astype(bf16)
-        coup_ref[yy, depth:, cols(q)] = im[yy * depth:(yy + 1) * depth].astype(bf16)
+    for u in parts:
+        coup_ref[u, 0:rows, cols(q)] = re[u * rows:(u + 1) * rows].astype(bf16)
+        coup_ref[u, rows:, cols(q)] = im[u * rows:(u + 1) * rows].astype(bf16)
         for k in range(len(others)):
-            coup_copy(yy, k, q).start()
+            coup_copy(u, k, q).start()
 
     x_swap(y).start()
     base_swap(y, plane * Y + y_peer).start()
@@ -363,17 +376,20 @@
             hop(1, yy, d)
     collect(1)
     trio = len(others) * part_width
-    for yy in range(Y):
-        got(coup_ref.at[yy, :, 0:trio], c_recv.at[yy])
-        re, im = complex_rows_here(coup_ref[yy], 1)
+    for u in parts:
+        got(coup_ref.at[u, :, 0:trio], c_recv.at[u])
+        re, im = complex_rows_here(coup_ref[u], 1)
+        here = slice(u % per * rows, (u % per + 1) * rows)
         for part, value in ((0, re), (1, im)):
-            start = g_ref[1, part, z * Y + yy, core]
-            g_ref[2, part, z * Y + yy, core] = (value + start.astype(f32)).astype(bf16)
-        near(2, yy)
+            start = g_ref[1, part, z * Y + u // per, core, here]
+            g_ref[2, part, z * Y + u // per, core, here] = (value + start.astype(f32)).astype(bf16)
+        near(2, u, outward)
+    for u in parts:
+        near(2, u, inner)
     share(2, 0)
-    for d in range(1, outer):
-        for yy in range(Y):
-            hop(2, yy, d)
+    for u in parts:
+        for d in range(2, outer):
+            hop(2, u, d)
     for d in range(1, outer):
         rest(2, d)
         share(2, d)
@@ -399,7 +415,14 @@
         return remote(f_ref.at[:, yy], whole_ref.at[:, :, cols(q)], f_send.at[0],
                       f_recv.at[0], dev(last, z, yy, core))
 
-    for j in range(outer):
+    handed, direct = range(outer // 2), range(outer // 2, outer)
+
+    def hand_copy(j):
+        spots = slice(j * tile, (j + 1) * tile)
+        return remote(d_ref.at[:, y_peer, :, spots], hand_ref.at[:, :, spots], d_send.at[0], hand_recv.at[j],
+                      dev(plane, z, y_peer, core))
+
+    for j in (direct[0], *handed, *direct[1:]):
         spots = slice(j * tile, (j + 1) * tile)
         dims = (((1,), (1,)), ((), ()))
         right = [g_ref[2, part, j * Y:(j + 1) * Y].reshape(tile, part_width) for part in range(2)]
@@ -410,8 +433,11 @@
 
         @pl.when(plane == last)
         def _():
-            d_copy(2, y_peer, j).start()
-            d_copy(0, y, j).start()
+            if j in handed:
+                hand_copy(j).start()
+            else:
+                d_copy(2, y_peer, j).start()
+                d_copy(0, y, j).start()
 
         @pl.when(plane != last)
         def _():
@@ -420,6 +446,13 @@
     @pl.when(plane == last)
     def _():
         f_copy(y_peer).start()
+        for j in handed:
+            spots = slice(j * tile, (j + 1) * tile)
+            got(hand_ref.at[:, :, spots], hand_recv.at[j])
+            for part in range(2):
+                d_ref[part, y, :, spots] = (d_ref[part, y, :, spots].astype(f32)
+                                            + hand_ref[part, :, spots].astype(f32)).astype(bf16)
+            d_copy(0, y, j).start()
 
     @pl.when(plane != last)
     def _():
@@ -460,12 +493,13 @@
 
     @pl.when(plane != last)
     def _():
-        for j in range(outer):
+        for j in (*direct, *handed):
             spots = slice(j * tile, (j + 1) * tile)
-            got(far_ref.at[:, :, :, spots], d_recv.at[j])
+            count = len(others) - (j in handed)
+            got(far_ref.at[0:count, :, :, spots], d_recv.at[j])
             for part in range(2):
                 total = d_ref.at[part][y, :, spots].astype(f32)
-                for k in range(len(others)):
+                for k in range(count):
                     total = total + far_ref[k, part, :, spots].astype(f32)
                 out_ref[:, part * width + j * tile:part * width + (j + 1) * tile] = (
                     x_ref.at[part][y, :, spots].astype(f32) + total.astype(bf16).astype(f32))
@@ -493,13 +527,14 @@
             pltpu.VMEM((1, sources), jnp.int32),
             pltpu.VMEM((3, 2, outer * Y, CORE, depth, quarter), bf16),
             pltpu.VMEM((2, Y, depth, width), bf16),
-            pltpu.VMEM((Y, 2 * depth, width), bf16),
+            pltpu.VMEM((SPLIT, 2 * Y * depth // SPLIT, width), bf16),
             pltpu.VMEM((2, Y, sources, width), bf16),
             pltpu.VMEM((2, Y, sources, width), bf16),
             pltpu.VMEM((2, Y, sources, quarter), bf16),
             pltpu.VMEM((2, sources, width), bf16),
             pltpu.VMEM((2, Y, sources, width), bf16),
             pltpu.VMEM((PLANES * Y - 1, 2, sources, width), bf16),
+            pltpu.VMEM((2, sources, width), bf16),
             pltpu.SemaphoreType.REGULAR((2,)),
             sem((3,)),
             sem((1,)),
@@ -507,18 +542,19 @@
             sem((1,)),
             sem((5,)),
             sem((1,)),
-            sem((3 * (outer - 1) * Y,)),
+            sem(((outer - 1) * (2 * Y + SPLIT),)),
             sem((1,)),
             sem((1,)),
             sem((3,)),
             sem((1,)),
-            sem((Y,)),
+            sem((SPLIT,)),
             sem((2,)),
             sem((2,)),
             sem((1,)),
             sem((1,)),
             sem((1,)),
             sem((outer,)),
+            sem((outer // 2,)),
         ],
         compiler_params=pltpu.CompilerParams(
             collective_id=0, has_side_effects=True, vmem_limit_bytes=32 << 20),

time: 47.8 us -> 46.1 us (0.964)
  Pallas kernels: 46.9 us -> 45.3 us
    pallas_call x1, Pallas kernels: 46.9 us -> 45.3 us  [pair_body(): pl.pallas_call(functools.partial(pair_kernel, outer), out_shape=pltpu.VME...]
where the time goes in v5:
time: 46.1 us; the launch traced here: 46 us
  Pallas kernels  45.3 us (98%)
  local copies, waits for them, and re-layouts  0.71 us (2%)
    pallas_call x1, Pallas kernels, pair_body(): pl.pallas_call(functools.partial(pair_kernel, outer), out_shape=pltpu.VME...  45.3 us

profile of v5, /device:TPU:0, one launch (start us, length us, event | category | flops | bytes accessed | tf_op | source)
XLA Modules:
  0.0 46.0 jit_solution(784627679950206669)
XLA Ops:
  0.0 45.3 %shard_map.55 = f32[32,2048]{1,0:T(8,128)S(1)} custom-call(bf16[1,64,2048]{2,1,0:T(8,128)(2,1)} %t_hbm.1, bf16[1,2,64,2048]{3,2,1,0:T(8,128)(2,1)} %r_hbm.1, bf16[32,2048]{1,0:T(8,128)(2,1)} %amp_hbm.1, s32[1,32]{1,0:T(1,128)} %bitcast.4, s32[1,32]{1,0:T(1,128)} %bitcast.5), custom_call_target="tpu_custom_call" | custom-call | tf_op jit(solution)/shard_map/pallas_call | solution.py:519
  45.3 0.7 %copy.7 = f32[1,32,2048]{2,1,0:T(8,128)} copy(f32[1,32,2048]{2,1,0:T(8,128)S(1)} %bitcast.3) | data formatting | bytes 524288

commit v6 on v5

--- a/solution.py
+++ b/solution.py
@@ -361,15 +361,15 @@
         ref = coup_ref.at[yy].at[:, cols(quarter)]
         return remote(ref, ref, c_send.at[0], c_recv.at[yy], dev(p, z, to_y, core))
 
-    re, im = complex_rows_here(left_ref[...].reshape(2 * Y * depth, width), 0)
-    for u in parts:
-        coup_ref[u, 0:rows, cols(q)] = re[u * rows:(u + 1) * rows].astype(bf16)
-        coup_ref[u, rows:, cols(q)] = im[u * rows:(u + 1) * rows].astype(bf16)
-        for k in range(len(others)):
-            coup_copy(u, k, q).start()
-
-    x_swap(y).start()
-    base_swap(y, plane * Y + y_peer).start()
+    for yy in range(Y):
+        re, im = complex_rows_here(left_ref[:, yy].reshape(2 * depth, width), 0)
+        for u in range(yy * per, (yy + 1) * per):
+            here = slice(u % per * rows, (u % per + 1) * rows)
+            coup_ref[u, 0:rows, cols(q)] = re[here].astype(bf16)
+            coup_ref[u, rows:, cols(q)] = im[here].astype(bf16)
+            for k in range(len(others)):
+                coup_copy(u, k, q).start()
+
 
     for yy in order:
         for d in range(2, outer):
@@ -384,12 +384,16 @@
             start = g_ref[1, part, z * Y + u // per, core, here]
             g_ref[2, part, z * Y + u // per, core, here] = (value + start.astype(f32)).astype(bf16)
         near(2, u, outward)
-    for u in parts:
+    x_swap(y).start()
+    base_swap(y, plane * Y + y_peer).start()
+    share(2, 0)
+    for u in parts[:len(parts) // 2]:
         near(2, u, inner)
-    share(2, 0)
     for u in parts:
         for d in range(2, outer):
             hop(2, u, d)
+        if u >= len(parts) // 2:
+            near(2, u, inner)
     for d in range(1, outer):
         rest(2, d)
         share(2, d)

time: 46.1 us -> 46 us (level)
  no operation moved by 1% of the time
where the time goes in v6:
time: 46 us; the launch traced here: 45.9 us
  Pallas kernels  45.1 us (98%)
  local copies, waits for them, and re-layouts  0.71 us (2%)
    pallas_call x1, Pallas kernels, pair_body(): pl.pallas_call(functools.partial(pair_kernel, outer), out_shape=pltpu.VME...  45.1 us

profile of v6, /device:TPU:0, one launch (start us, length us, event | category | flops | bytes accessed | tf_op | source)
XLA Modules:
  0.0 45.9 jit_solution(3511331800952105018)
XLA Ops:
  0.0 45.1 %shard_map.55 = f32[32,2048]{1,0:T(8,128)S(1)} custom-call(bf16[1,64,2048]{2,1,0:T(8,128)(2,1)} %t_hbm.1, bf16[1,2,64,2048]{3,2,1,0:T(8,128)(2,1)} %r_hbm.1, bf16[32,2048]{1,0:T(8,128)(2,1)} %amp_hbm.1, s32[1,32]{1,0:T(1,128)} %bitcast.4, s32[1,32]{1,0:T(1,128)} %bitcast.5), custom_call_target="tpu_custom_call" | custom-call | tf_op jit(solution)/shard_map/pallas_call | solution.py:523
  45.2 0.7 %copy.7 = f32[1,32,2048]{2,1,0:T(8,128)} copy(f32[1,32,2048]{2,1,0:T(8,128)S(1)} %bitcast.3) | data formatting | bytes 524288

commit v7 on v6

--- a/solution.py
+++ b/solution.py
@@ -243,25 +243,24 @@
                 remote(ref, ref, relay_send.at[0], z_sem(m, s - onward, yy),
                        dev(plane, z + onward, y, core)).start()
 
-    def rest(m, d):
-        for s in (d, -d):
-            @pl.when(valid(z + s) & ~onward_ok(s))
-            def _():
-                for yy in range(Y) if m < 2 else parts:
-                    got(unit(m, z + s, yy), z_sem(m, s, yy))
-
-    def chunk(m, zz, cc):
-        return g_ref.at[m].at[:, pl.ds(zz * Y, Y), cc]
-
-    def core_copy(m, zz, cc):
-        return remote(chunk(m, zz, cc), chunk(m, zz, cc), core_send.at[0], core_recv.at[m],
-                      dev(plane, z, y, c_peer))
-
-    def share(m, d):
+    def units(m):
+        return order if m < 2 else parts
+
+    def share(m, d, only=None):
         for s in ((d, -d) if d else (0,)):
             @pl.when(valid(z + s))
             def _():
-                core_copy(m, z + s, core).start()
+                for u in units(m) if only is None else (only,):
+                    ref = unit(m, z + s, u)
+                    remote(ref, ref, core_send.at[0], core_recv.at[m], dev(plane, z, y, c_peer)).start()
+
+    def rest(m, d):
+        for u in units(m):
+            for s in (d, -d):
+                @pl.when(valid(z + s) & ~onward_ok(s))
+                def _():
+                    got(unit(m, z + s, u), z_sem(m, s, u))
+            share(m, d, u)
 
     def finish(m):
         got(g_ref.at[m].at[:, :, c_peer], core_recv.at[m])
@@ -269,7 +268,6 @@
     def collect(m):
         for d in range(1, outer):
             rest(m, d)
-            share(m, d)
         finish(m)
 
     def side(m, part):
@@ -344,7 +342,6 @@
 
     for d in range(1, outer):
         rest(0, d)
-        share(0, d)
     got(left_ref.at[:, y_peer], left_recv.at[len(left_units)])
     finish(0)
 
@@ -396,7 +393,6 @@
             near(2, u, inner)
     for d in range(1, outer):
         rest(2, d)
-        share(2, d)
     x_swap(y_peer).wait_recv()
     base_swap(y_peer, q).wait_recv()
     finish(2)

time: 46 us -> 45.8 us (level)
  no operation moved by 1% of the time
where the time goes in v7:
time: 45.8 us; the launch traced here: 45.6 us
  Pallas kernels  44.9 us (98%)
  local copies, waits for them, and re-layouts  0.71 us (2%)
    pallas_call x1, Pallas kernels, pair_body(): pl.pallas_call(functools.partial(pair_kernel, outer), out_shape=pltpu.VME...  44.9 us

profile of v7, /device:TPU:0, one launch (start us, length us, event | category | flops | bytes accessed | tf_op | source)
XLA Modules:
  0.0 45.6 jit_solution(3080112750026726167)
XLA Ops:
  0.0 44.9 %shard_map.55 = f32[32,2048]{1,0:T(8,128)S(1)} custom-call(bf16[1,64,2048]{2,1,0:T(8,128)(2,1)} %t_hbm.1, bf16[1,2,64,2048]{3,2,1,0:T(8,128)(2,1)} %r_hbm.1, bf16[32,2048]{1,0:T(8,128)(2,1)} %amp_hbm.1, s32[1,32]{1,0:T(1,128)} %bitcast.4, s32[1,32]{1,0:T(1,128)} %bitcast.5), custom_call_target="tpu_custom_call" | custom-call | tf_op jit(solution)/shard_map/pallas_call | solution.py:519
  44.9 0.7 %copy.7 = f32[1,32,2048]{2,1,0:T(8,128)} copy(f32[1,32,2048]{2,1,0:T(8,128)S(1)} %bitcast.3) | data formatting | bytes 524288

commit v8 on v7

--- a/solution.py
+++ b/solution.py
@@ -86,7 +86,7 @@
     z, y, core = me // (Y * CORE), (me // CORE) % Y, me % CORE
     last = PLANES - 1
     depth = t_hbm.shape[1]
-    half = depth // 2
+    half = depth // 4
     width = t_hbm.shape[2] // 2
     part_width = width // (PLANES * Y)
     sources = amp_hbm.shape[0]
@@ -141,7 +141,7 @@
     def piece_wait(m, yy):
         got(unit(m, z, yy), in_recv.at[m * Y + yy])
 
-    left_units = [(part, h) for part in range(2) for h in range(2)]
+    left_units = [(part, h) for part in range(2) for h in range(4)]
 
     def left_rows(part, h, yy):
         return left_ref.at[part].at[yy, h * half:(h + 1) * half]
@@ -290,14 +290,13 @@
         piece_wait(0, y_peer)
         near(0, y_peer)
         share(0, 0)
-        piece_wait(1, y)
-        near(1, y, lambda s: ~relays_to(s))
         hop(0, y, 2)
         hop(0, y_peer, 2)
         for yy in order:
             for d in range(3, outer):
                 hop(0, yy, d)
-        near(1, y, relays_to)
+        piece_wait(1, y)
+        near(1, y)
         piece_wait(1, y_peer)
         near(1, y_peer)
         share(1, 0)
@@ -331,7 +330,8 @@
         for u, (part, h) in enumerate(left_units):
             got(left_rows(part, h, y), left_recv.at[u])
             left_relay(u, part, h).start()
-            hop(0, *hops[u])
+            if u % 2:
+                hop(0, *hops[u // 2])
         for yy in order:
             for d in range(3, outer):
                 hop(0, yy, d)
@@ -540,7 +540,7 @@
             sem((1,)),
             sem((2 * Y + 1,)),
             sem((1,)),
-            sem((5,)),
+            sem((9,)),
             sem((1,)),
             sem(((outer - 1) * (2 * Y + SPLIT),)),
             sem((1,)),

time: 45.8 us -> 45.8 us (level)
  no operation moved by 1% of the time
where the time goes in v8:
time: 45.8 us; the launch traced here: 45.6 us
  Pallas kernels  44.9 us (98%)
  local copies, waits for them, and re-layouts  0.71 us (2%)
    pallas_call x1, Pallas kernels, pair_body(): pl.pallas_call(functools.partial(pair_kernel, outer), out_shape=pltpu.VME...  44.9 us

profile of v8, /device:TPU:0, one launch (start us, length us, event | category | flops | bytes accessed | tf_op | source)
XLA Modules:
  0.0 45.6 jit_solution(12201753874744347635)
XLA Ops:
  0.0 44.9 %shard_map.55 = f32[32,2048]{1,0:T(8,128)S(1)} custom-call(bf16[1,64,2048]{2,1,0:T(8,128)(2,1)} %t_hbm.1, bf16[1,2,64,2048]{3,2,1,0:T(8,128)(2,1)} %r_hbm.1, bf16[32,2048]{1,0:T(8,128)(2,1)} %amp_hbm.1, s32[1,32]{1,0:T(1,128)} %bitcast.4, s32[1,32]{1,0:T(1,128)} %bitcast.5), custom_call_target="tpu_custom_call" | custom-call | tf_op jit(solution)/shard_map/pallas_call | solution.py:519
  44.9 0.7 %copy.7 = f32[1,32,2048]{2,1,0:T(8,128)} copy(f32[1,32,2048]{2,1,0:T(8,128)S(1)} %bitcast.3) | data formatting | bytes 524288

commit v9 on v7

--- a/solution.py
+++ b/solution.py
@@ -290,14 +290,13 @@
         piece_wait(0, y_peer)
         near(0, y_peer)
         share(0, 0)
-        piece_wait(1, y)
-        near(1, y, lambda s: ~relays_to(s))
         hop(0, y, 2)
         hop(0, y_peer, 2)
         for yy in order:
             for d in range(3, outer):
                 hop(0, yy, d)
-        near(1, y, relays_to)
+        piece_wait(1, y)
+        near(1, y)
         piece_wait(1, y_peer)
         near(1, y_peer)
         share(1, 0)

time: 45.8 us -> 45.8 us (level)
  no operation moved by 1% of the time
where the time goes in v9:
time: 45.8 us; the launch traced here: 45.6 us
  Pallas kernels  44.9 us (98%)
  local copies, waits for them, and re-layouts  0.71 us (2%)
    pallas_call x1, Pallas kernels, pair_body(): pl.pallas_call(functools.partial(pair_kernel, outer), out_shape=pltpu.VME...  44.9 us

profile of v9, /device:TPU:0, one launch (start us, length us, event | category | flops | bytes accessed | tf_op | source)
XLA Modules:
  0.0 45.6 jit_solution(15038328517937500722)
XLA Ops:
  0.0 44.9 %shard_map.55 = f32[32,2048]{1,0:T(8,128)S(1)} custom-call(bf16[1,64,2048]{2,1,0:T(8,128)(2,1)} %t_hbm.1, bf16[1,2,64,2048]{3,2,1,0:T(8,128)(2,1)} %r_hbm.1, bf16[32,2048]{1,0:T(8,128)(2,1)} %amp_hbm.1, s32[1,32]{1,0:T(1,128)} %bitcast.4, s32[1,32]{1,0:T(1,128)} %bitcast.5), custom_call_target="tpu_custom_call" | custom-call | tf_op jit(solution)/shard_map/pallas_call | solution.py:518
  44.9 0.7 %copy.7 = f32[1,32,2048]{2,1,0:T(8,128)} copy(f32[1,32,2048]{2,1,0:T(8,128)S(1)} %bitcast.3) | data formatting | bytes 524288
